TPU v7x, 256 devices: a whole 4x4x8 slice. The times are simulated.
256 devices in a mesh: dp: 8 (over x, core), expert: 32 (over y, z).
Axes of the slice: x: 4, y: 4, z: 8, core: 2. Of those that a mesh axis runs over, the one named last changes fastest.
Arguments:
- tokens: bfloat16 [4096, 4096], P(('dp', 'expert')), may hold values from -6 to 6
- routes: int32 [4096, 8], P(('dp', 'expert')), may hold values from 0 to 127, all different within a row; in each aligned block of 16 rows (0 to 15, 16 to 31, ...) at most 2 rows name the same one
- route_gates: float32 [4096, 8], P(('dp', 'expert')), may hold values from 0.02 to 0.5
- placement: int32 [128], replicated, may hold values from 0 to 127, each once
- swap_flags: int32 [128], replicated, may hold values from 0 to 1, as said below
- gate_weight: bfloat16 [32, 4096, 3072], P('expert', None, 'dp'), may hold values from -0.09375 to 0.09375
- up_weight: bfloat16 [32, 4096, 3072], P('expert', None, 'dp'), may hold values from -0.09375 to 0.09375
- down_weight: bfloat16 [32, 3072, 4096], P('expert', 'dp'), may hold values from -0.21875 to 0.21875
Outputs:
- layer_out: bfloat16 [4096, 4096], P(('dp', 'expert'))
Inputs may be any that keep to these rules, and one draw needn't show every extreme that they name: `routes`: each row names 8 different experts; among the 16 rows of one device no expert is named more than 2 times, a bound that some block reaches. `placement`: A permutation of the 128 positions. swap_flags[P] equals swap_flags[(P + 64) mod 128].
All inputs are finite; a program needn't handle non-finite values.
Results may differ from a plain program's by a relative error of at most 0.0065.
Values may be sent and summed in bfloat16 or wider, within the bound.
A program may use at most 128 MiB of HBM per device.

v0:
```python
import jax
import jax.numpy as jnp
from jax import lax
from jax.sharding import PartitionSpec as P


def passed_along(value, axis, by):
    peers = lax.axis_size(axis)
    return lax.ppermute(value, axis, [(i, (i + by) % peers) for i in range(peers)])


def expert_block(received, w_gate, w_up, w_down):
    gate_act = jnp.dot(received, w_gate, preferred_element_type=jnp.float32)
    up_act = jnp.dot(received, w_up, preferred_element_type=jnp.float32)
    hidden = (jax.nn.silu(gate_act) * up_act).astype(jnp.bfloat16)
    return jnp.dot(hidden, w_down, preferred_element_type=jnp.float32).astype(jnp.bfloat16)


def on_device(
    tokens, routes, route_gates, placement, swap_flags, gate_weight, up_weight, down_weight
):
    tok_dev = tokens.shape[0]
    features = tokens.shape[1]
    route_count = routes.shape[1]
    columns = lax.axis_size("expert")
    replicas = lax.axis_size("dp")
    slot_count = replicas // 2
    experts = slot_count * columns
    capacity = 2 * tok_dev * route_count // experts
    lane_count = slot_count * columns * capacity
    expert_ids = jnp.arange(experts, dtype=jnp.int32)
    flat_routes = routes.reshape(-1)
    matches = (flat_routes[:, None] == expert_ids[None, :]).astype(jnp.int32)
    target = jnp.sum(matches * placement[None, :], axis=1)
    ranking = jnp.sum(matches * (jnp.cumsum(matches, axis=0) - 1), axis=1)
    w_gate = gate_weight[0]
    w_up = up_weight[0]
    w_down = down_weight[0]
    partner_blocks = passed_along((w_gate, w_up, w_down), "expert", columns // 2)
    own_position = lax.axis_index("expert") * slot_count + lax.axis_index("dp") // 2
    own_flag = jnp.sum(jnp.where(expert_ids == own_position, swap_flags, 0))
    unswapped = own_flag == 0
    w_gate = jnp.where(unswapped, w_gate, partner_blocks[0])
    w_up = jnp.where(unswapped, w_up, partner_blocks[1])
    w_down = jnp.where(unswapped, w_down, partner_blocks[2])
    column = target // slot_count
    slot_id = target % slot_count
    lane_index = (slot_id * columns + column) * capacity + ranking
    pair_row = jnp.arange(tok_dev * route_count, dtype=jnp.int32) // route_count
    lane_hit = (jnp.arange(lane_count, dtype=jnp.int32)[:, None] == lane_index[None, :]).astype(
        jnp.float32
    )
    row_hit = (jnp.arange(tok_dev, dtype=jnp.int32)[:, None] == pair_row[None, :]).astype(
        jnp.float32
    )
    selector = jnp.dot(lane_hit, row_hit.T, precision=lax.Precision.HIGHEST).astype(jnp.bfloat16)
    combine = jnp.dot(
        row_hit * route_gates.reshape(-1)[None, :], lane_hit.T, precision=lax.Precision.HIGHEST
    )
    outgoing = jnp.dot(selector, tokens, preferred_element_type=jnp.float32).astype(jnp.bfloat16)
    outgoing = outgoing.reshape(slot_count, columns, capacity, features)
    doubled = jnp.repeat(outgoing, 2, axis=0)
    arrived = lax.all_to_all(
        lax.all_to_all(doubled, "dp", split_axis=0, concat_axis=0, tiled=True),
        "expert",
        split_axis=1,
        concat_axis=1,
        tiled=True,
    )
    partial_value = expert_block(arrived.reshape(-1, features), w_gate, w_up, w_down)
    partial_value = partial_value.reshape(replicas, columns, capacity, features)
    returned = lax.all_to_all(
        lax.all_to_all(partial_value, "dp", split_axis=0, concat_axis=0, tiled=True),
        "expert",
        split_axis=1,
        concat_axis=1,
        tiled=True,
    )
    halves = returned.reshape(slot_count, 2, columns, capacity, features)
    summed = (halves[:, 0].astype(jnp.float32) + halves[:, 1].astype(jnp.float32)).astype(
        jnp.bfloat16
    )
    expert_rows = summed.reshape(lane_count, features)
    layer_out = jnp.dot(combine, expert_rows.astype(jnp.float32), precision=lax.Precision.HIGHEST)
    return layer_out.astype(jnp.bfloat16)


def solution(mesh):
    return jax.shard_map(
        on_device,
        mesh=mesh,
        in_specs=(
            P(("dp", "expert"), None),
            P(("dp", "expert"), None),
            P(("dp", "expert"), None),
            P(),
            P(),
            P("expert", None, "dp"),
            P("expert", None, "dp"),
            P("expert", "dp", None),
        ),
        out_specs=P(("dp", "expert"), None),
        check_vma=False,
    )
```

profile of v0, /device:TPU:2, one launch (start us, length us, event | category | flops | bytes accessed | tf_op | source)
XLA Modules:
  0.0 529.1 jit_solution(3678586884088264812)
XLA Ops:
  0.0 0.0 copy-start
  0.0 0.8 copy.25
  0.8 0.1 eq.62
  0.9 0.1 fusion.12
  1.0 0.2 reduce_window_sum.11
  1.2 0.8 select_reduce_fusion.1
  2.0 0.1 convolution_convert_fusion.3
  2.2 0.0 copy-done
  2.2 2.1 convolution_convert_fusion.1
  4.2 3.2 reshape.72
  7.4 7.1 %broadcast_in_dim.4 = bf16[4,2,32,2,4096]{4,3,2,1,0:T(2,128)(2,1)} broadcast(bf16[4,32,2,4096]{3,2,1,0:T(2,128)(2,1)S(1)} %reshape.72), dimensions={0,2,3,4} | broadcast | bytes 6291456 | tf_op jit(solution)/shard_map/broadcast_in_dim | solution.py:62
  14.5 54.7 %all_to_all.20 = bf16[8,32,2,4096]{3,2,1,0:T(2,128)(2,1)S(1)} all-to-all(bf16[8,32,2,4096]{3,2,1,0:T(2,128)(2,1)} %bitcast.25), channel_id=1, replica_groups=mesh['dp'=8,'expert'=32] {'dp'}, dimensions={0} | all-to-all | bytes 8388608 | tf_op jit(solution)/shard_map/all_to_all | solution.py:64
  69.2 6.1 %copy.26 = bf16[8,32,2,4096]{3,2,0,1:T(2,128)(2,1)} copy(bf16[8,32,2,4096]{3,2,1,0:T(2,128)(2,1)S(1)} %all_to_all.20) | data formatting | bytes 8388608 | tf_op jit(solution)/shard_map/all_to_all | solution.py:64
  75.4 0.0 copy-start.6
  75.4 10.7 %all-to-all-start.1 = ((bf16[8,32,2,4096]{3,2,0,1:T(2,128)(2,1)}), bf16[8,32,2,4096]{3,2,0,1:T(2,128)(2,1)}, u32[]{:S(2)}, u32[]{:S(2)}) async-start(bf16[8,32,2,4096]{3,2,0,1:T(2,128)(2,1)} %copy.26), calls=%async_computation.1 | async-start | bytes 8388608 | tf_op jit(solution)/shard_map/all_to_all | solution.py:63
  86.1 3.3 collective-permute-start.1
  89.4 0.3 collective-permute-start
  89.7 3.2 collective-permute-start.2
  92.9 0.0 copy-done.6
  92.9 0.6 fusion.20
  94.2 85.7 %all-to-all-done.1 = bf16[8,32,2,4096]{3,2,0,1:T(2,128)(2,1)} async-done(((bf16[8,32,2,4096]{3,2,0,1:T(2,128)(2,1)}), bf16[8,32,2,4096]{3,2,0,1:T(2,128)(2,1)}, u32[]{:S(2)}, u32[]{:S(2)}) %all-to-all-start.1) | async-done | bytes 4194336 | tf_op jit(solution)/shard_map/all_to_all | solution.py:63
  179.9 10.0 %copy.27 = bf16[8,32,2,4096]{3,2,1,0:T(2,128)(2,1)} copy(bf16[8,32,2,4096]{3,2,0,1:T(2,128)(2,1)} %all-to-all-done.1) | data formatting | bytes 8388608 | tf_op jit(solution)/shard_map/all_to_all | solution.py:63
  189.9 7.2 %reshape.74 = bf16[512,4096]{1,0:T(8,128)(2,1)} reshape(bf16[8,32,2,4096]{3,2,1,0:T(2,128)(2,1)} %copy.27) | data formatting | bytes 8388608 | tf_op jit(solution)/shard_map/reshape | solution.py:70
  197.1 0.0 copy-start.2
  197.1 0.0 copy-start.4
  197.1 7.8 %collective-permute-done.1 = bf16[4096,384]{1,0:T(8,128)(2,1)} collective-permute-done((bf16[4096,384]{1,0:T(8,128)(2,1)}, bf16[4096,384]{1,0:T(8,128)(2,1)}, u32[]{:S(2)}, u32[]{:S(2)}) %collective-permute-start.1) | collective-permute-done | bytes 3145760 | tf_op jit(solution)/shard_map/ppermute | solution.py:9
  204.9 6.4 %fusion.1 = f32[512,384]{1,0:T(8,128)S(1)} fusion(bf16[512,4096]{1,0:T(8,128)(2,1)} %reshape.74, bf16[4096,384]{1,0:T(8,128)(2,1)} %collective-permute-done.1, pred[]{:T(512)S(6)} %eq.70, bf16[1,4096,384]{2,1,0:T(8,128)(2,1)} %param.14), kind=kOutput, calls=%fused_computation.5 | convolution fusion | flops 1612185600 | bytes 11272193 | tf_op jit(solution)/shard_map/dot_general | solution.py:14
  211.3 0.0 copy-start.5
  211.3 61.0 %collective-permute-done = bf16[4096,384]{1,0:T(8,128)(2,1)} collective-permute-done((bf16[4096,384]{1,0:T(8,128)(2,1)}, bf16[4096,384]{1,0:T(8,128)(2,1)}, u32[]{:S(2)}, u32[]{:S(2)}) %collective-permute-start) | collective-permute-done | bytes 3145760 | tf_op jit(solution)/shard_map/ppermute | solution.py:9
  272.3 0.0 copy-done.2
  272.3 0.0 copy-done.4
  272.3 4.3 fusion.3
  276.6 61.3 %collective-permute-done.2 = bf16[384,4096]{1,0:T(8,128)(2,1)} collective-permute-done((bf16[384,4096]{1,0:T(8,128)(2,1)}, bf16[384,4096]{1,0:T(8,128)(2,1)}, u32[]{:S(2)}, u32[]{:S(2)}) %collective-permute-start.2) | collective-permute-done | bytes 3145760 | tf_op jit(solution)/shard_map/ppermute | solution.py:9
  337.9 0.0 copy-done.5
  337.9 6.2 %convolution_convert_fusion = bf16[512,4096]{1,0:T(8,128)(2,1)} fusion(bf16[384,4096]{1,0:T(8,128)(2,1)} %collective-permute-done.2, pred[]{:T(512)S(6)} %eq.70, f32[512,384]{1,0:T(8,128)S(1)} %fusion.1, f32[512,384]{1,0:T(8,128)S(1)} %fusion.3, bf16[1,384,4096]{2,1,0:T(8,128)(2,1)S(1)} %copy-done.5), kind=kOutput, calls=%fused_computation | convolution fusion | flops 1615462400 | bytes 12058625 | tf_op jit(solution)/shard_map/dot_general | solution.py:16
  344.1 7.7 %reshape.75 = bf16[8,32,2,4096]{3,2,1,0:T(2,128)(2,1)} reshape(bf16[512,4096]{1,0:T(8,128)(2,1)} %convolution_convert_fusion) | data formatting | bytes 8388608 | tf_op jit(solution)/shard_map/reshape | solution.py:71
  351.8 53.9 %all_to_all.21 = bf16[8,32,2,4096]{3,2,1,0:T(2,128)(2,1)S(1)} all-to-all(bf16[8,32,2,4096]{3,2,1,0:T(2,128)(2,1)} %reshape.75), channel_id=1, replica_groups=mesh['dp'=8,'expert'=32] {'dp'}, dimensions={0} | all-to-all | bytes 8388608 | tf_op jit(solution)/shard_map/all_to_all | solution.py:73
  405.7 6.1 %copy.28 = bf16[8,32,2,4096]{3,2,0,1:T(2,128)(2,1)} copy(bf16[8,32,2,4096]{3,2,1,0:T(2,128)(2,1)S(1)} %all_to_all.21) | data formatting | bytes 8388608 | tf_op jit(solution)/shard_map/all_to_all | solution.py:73
  411.8 0.0 copy-start.3
  411.8 7.1 %all-to-all-start.3 = ((bf16[8,32,2,4096]{3,2,0,1:T(2,128)(2,1)}), bf16[8,32,2,4096]{3,2,0,1:T(2,128)(2,1)}, u32[]{:S(2)}, u32[]{:S(2)}) async-start(bf16[8,32,2,4096]{3,2,0,1:T(2,128)(2,1)} %copy.28), calls=%async_computation.3 | async-start | bytes 8388608 | tf_op jit(solution)/shard_map/all_to_all | solution.py:72
  418.9 0.0 copy-done.3
  418.9 0.1 copy.24
  419.0 0.1 mul.49
  419.1 0.1 fusion.9
  419.2 96.3 %all-to-all-done.3 = bf16[8,32,2,4096]{3,2,0,1:T(2,128)(2,1)} async-done(((bf16[8,32,2,4096]{3,2,0,1:T(2,128)(2,1)}), bf16[8,32,2,4096]{3,2,0,1:T(2,128)(2,1)}, u32[]{:S(2)}, u32[]{:S(2)}) %all-to-all-start.3) | async-done | bytes 4194336 | tf_op jit(solution)/shard_map/all_to_all | solution.py:72
  515.5 5.2 fusion.26
  520.7 0.0 copy-start.1
  520.8 2.9 add_convert_fusion
  523.7 2.2 convert_element_type.46
  525.9 3.2 convolution_convert_fusion.2
  529.1 0.0 copy-done.1
  (1 shorter events, 0.0 us)
Async XLA Ops:
  0.0 2.2 copy-start
  75.4 17.6 %copy-start.6 = (s32[128]{0:T(128)S(1)}, s32[128]{0:T(128)}, u32[]{:S(2)}) copy-start(s32[128]{0:T(128)} %param.12) | copy-start | bytes 1540
  75.4 104.6 %all-to-all-start.1 = ((bf16[8,32,2,4096]{3,2,0,1:T(2,128)(2,1)}), bf16[8,32,2,4096]{3,2,0,1:T(2,128)(2,1)}, u32[]{:S(2)}, u32[]{:S(2)}) async-start(bf16[8,32,2,4096]{3,2,0,1:T(2,128)(2,1)} %copy.26), calls=%async_computation.1 | async-start | bytes 8388608 | tf_op jit(solution)/shard_map/all_to_all | solution.py:63
  86.1 118.8 %collective-permute-start.1 = (bf16[4096,384]{1,0:T(8,128)(2,1)}, bf16[4096,384]{1,0:T(8,128)(2,1)}, u32[]{:S(2)}, u32[]{:S(2)}) collective-permute-start(bf16[4096,384]{1,0:T(8,128)(2,1)} %bitcast.26), channel_id=1, source_target_pairs={{0,16},{1,17},{2,18},{3,19},{4,20},{5,21},{6,22},{7,23},{8,24},{9,... | collective-permute-start | bytes 9437192 | tf_op jit(solution)/shard_map/ppermute | solution.py:9
  89.4 182.9 %collective-permute-start = (bf16[4096,384]{1,0:T(8,128)(2,1)}, bf16[4096,384]{1,0:T(8,128)(2,1)}, u32[]{:S(2)}, u32[]{:S(2)}) collective-permute-start(bf16[4096,384]{1,0:T(8,128)(2,1)} %bitcast.27), channel_id=1, source_target_pairs={{0,16},{1,17},{2,18},{3,19},{4,20},{5,21},{6,22},{7,23},{8,24},{9,... | collective-permute-start | bytes 9437192 | tf_op jit(solution)/shard_map/ppermute | solution.py:9
  89.7 248.2 %collective-permute-start.2 = (bf16[384,4096]{1,0:T(8,128)(2,1)}, bf16[384,4096]{1,0:T(8,128)(2,1)}, u32[]{:S(2)}, u32[]{:S(2)}) collective-permute-start(bf16[384,4096]{1,0:T(8,128)(2,1)} %bitcast.28), channel_id=1, source_target_pairs={{0,16},{1,17},{2,18},{3,19},{4,20},{5,21},{6,22},{7,23},{8,24},{9,... | collective-permute-start | bytes 9437192 | tf_op jit(solution)/shard_map/ppermute | solution.py:9
  197.1 75.2 %copy-start.2 = (bf16[512,4096]{1,0:T(8,128)(2,1)S(1)}, bf16[512,4096]{1,0:T(8,128)(2,1)}, u32[]{:S(2)}) copy-start(bf16[512,4096]{1,0:T(8,128)(2,1)} %reshape.74) | copy-start | bytes 12582916
  197.1 75.2 %copy-start.4 = (bf16[1,4096,384]{2,1,0:T(8,128)(2,1)S(1)}, bf16[1,4096,384]{2,1,0:T(8,128)(2,1)}, u32[]{:S(2)}) copy-start(bf16[1,4096,384]{2,1,0:T(8,128)(2,1)} %param.13) | copy-start | bytes 9437188
  211.3 126.6 %copy-start.5 = (bf16[1,384,4096]{2,1,0:T(8,128)(2,1)S(1)}, bf16[1,384,4096]{2,1,0:T(8,128)(2,1)}, u32[]{:S(2)}) copy-start(bf16[1,384,4096]{2,1,0:T(8,128)(2,1)} %param.15) | copy-start | bytes 9437188
  411.8 7.1 %copy-start.3 = (f32[16,8]{0,1:T(8,128)S(1)}, f32[16,8]{0,1:T(8,128)}, u32[]{:S(2)}) copy-start(f32[16,8]{0,1:T(8,128)} %param.10) | copy-start | bytes 1540
  411.8 103.7 %all-to-all-start.3 = ((bf16[8,32,2,4096]{3,2,0,1:T(2,128)(2,1)}), bf16[8,32,2,4096]{3,2,0,1:T(2,128)(2,1)}, u32[]{:S(2)}, u32[]{:S(2)}) async-start(bf16[8,32,2,4096]{3,2,0,1:T(2,128)(2,1)} %copy.28), calls=%async_computation.3 | async-start | bytes 8388608 | tf_op jit(solution)/shard_map/all_to_all | solution.py:72
  520.7 8.3 %copy-start.1 = (bf16[16,4096]{1,0:T(8,128)(2,1)S(1)}, bf16[16,4096]{1,0:T(8,128)(2,1)}, u32[]{:S(2)}) copy-start(bf16[16,4096]{1,0:T(8,128)(2,1)} %param.8) | copy-start | bytes 393220
where the time goes:
time: 530 us; the launch traced here: 529 us
  waiting for transfers between devices  312 us (59%)
  blocking collectives  109 us (21%)
  local copies, waits for them, and re-layouts  55.8 us (11%)
  starting transfers between devices  24.6 us (5%)
  matrix products  22.4 us (4%)
    ppermute x3, waiting for transfers between devices, passed_along(): lax.ppermute(value, axis, [(i, (i + by) % peers) for i in range(peers)])  130 us
    all_to_all x1, waiting for transfers between devices, on_device(): lax.all_to_all(lax.all_to_all(partial_value, 'dp', split_axis=0, concat_a...  96.3 us
    all_to_all x1, waiting for transfers between devices, on_device(): lax.all_to_all(lax.all_to_all(doubled, 'dp', split_axis=0, concat_axis=0,...  85.7 us
    all_to_all x1, blocking collectives, on_device(): lax.all_to_all(doubled, 'dp', split_axis=0, concat_axis=0, tiled=True)  54.7 us
    all_to_all x1, blocking collectives, on_device(): lax.all_to_all(partial_value, 'dp', split_axis=0, concat_axis=0, tiled=True)  53.9 us
    all_to_all x1, starting transfers between devices, on_device(): lax.all_to_all(lax.all_to_all(doubled, 'dp', split_axis=0, concat_axis=0,...  10.7 us
  transfers between devices with their start and end apart: 5, of which 5 were waited for; matrix products, arithmetic and copies ran while one was open for 5% of the time, Pallas kernels for 0%

commit v1 on v0

v1 whole, which is shorter than its diff:
```python
import functools

import jax
import jax.numpy as jnp
from jax import lax
from jax.experimental import pallas as pl
from jax.experimental.pallas import tpu as pltpu
from jax.sharding import PartitionSpec as P

NX, NY, NZ = 4, 4, 8
PLANE = NX * NY
ROWS = 16
WIDE = 4096
HALF = 384
CHUNKS = 4
CW = WIDE // CHUNKS
TILE = 256
MESH = pl.DeviceIdType.MESH
F32 = jnp.float32
BF16 = jnp.bfloat16


def dot(a, b):
    return jnp.dot(a, b, preferred_element_type=F32)


def kernel(
    tokens, routes, gates, placement, flags, w_gate, w_up, w_down, out,
    tok, meta, sel, comb, comb_t, away, rows, w_in, w_out, acc, hid,
    mine, theirs, got, ret, back, part, hop_out, hop_in,
    w_sem, meta_send, meta_recv, ag_send, ag_recv, go_send, go_recv, sib_send, sib_recv,
    half_send, half_recv, back_send, back_recv, rs_send, rs_recv,
):
    dp = lax.axis_index("dp")
    ex = lax.axis_index("expert")
    x, core = dp // 2, dp % 2
    y, z = ex // NZ, ex % NZ
    sibling = (x * 2 + (1 - core), ex)

    def along_z(by):
        return (dp, y * NZ + (z + by + NZ) % NZ)

    def in_plane(dx, dy):
        return (((x + dx + NX) % NX) * 2 + core, ((y + dy + NY) % NY) * NZ + z)

    def remote(src, dst, send, recv, device):
        return pltpu.make_async_remote_copy(
            src_ref=src, dst_ref=dst, send_sem=send, recv_sem=recv, device_id=device, device_id_type=MESH
        )

    barrier = pltpu.get_barrier_semaphore()
    for i in range(1, NZ):
        pl.semaphore_signal(barrier, inc=1, device_id=along_z(i), device_id_type=MESH)
    for d in range(1, PLANE):
        pl.semaphore_signal(barrier, inc=1, device_id=in_plane(d % NX, d // NX), device_id_type=MESH)
    pl.semaphore_signal(barrier, inc=1, device_id=sibling, device_id_type=MESH)

    loads = (
        pltpu.make_async_copy(w_gate.at[0], w_in.at[:, pl.ds(0, HALF)], w_sem.at[0]),
        pltpu.make_async_copy(w_up.at[0], w_in.at[:, pl.ds(HALF, HALF)], w_sem.at[1]),
        pltpu.make_async_copy(w_down.at[0], w_out, w_sem.at[2]),
    )
    for load in loads:
        load.start()

    for c in range(CHUNKS):
        tok[c, 0] = tokens[:, c * CW:(c + 1) * CW]
    meta[0] = jnp.zeros((ROWS, 128), F32)
    meta[0, :, 0:8] = routes[...].astype(F32)
    meta[0, :, 8:16] = gates[...]

    pl.semaphore_wait(barrier, NZ - 1 + PLANE - 1 + 1)

    meta_copies = [
        remote(meta.at[0], meta.at[i], meta_send.at[i], meta_recv.at[i], along_z(-i)) for i in range(1, NZ)
    ]
    for copy in meta_copies:
        copy.start()

    def ag(c, src, dst):
        by = -1 if src < dst else 1
        return remote(tok.at[c, src % NZ], tok.at[c, dst], ag_send.at[c, dst], ag_recv.at[c, dst], along_z(by))

    def ag_steps(c):
        down, up = (4, 3) if c % 2 == 0 else (3, 4)
        return [(i - 1, i) for i in range(1, down + 1)], [(NZ - i + 1, NZ - i) for i in range(1, up + 1)]

    started = {}

    def ag_start(c, src, dst):
        started[(c, dst)] = ag(c, src, dst)
        started[(c, dst)].start()

    for c in range(CHUNKS):
        for way in ag_steps(c):
            ag_start(c, *way[0])

    lane = lax.broadcasted_iota(jnp.int32, (128, 128), 1)
    line = lax.broadcasted_iota(jnp.int32, (128, 128), 0)
    lane_f = lane.astype(F32)
    placed = jnp.broadcast_to(placement[...].astype(F32), (128, 128)).T
    flag = jnp.sum(
        jnp.where(placed == lane_f, jnp.broadcast_to(flags[...].astype(F32), (128, 128)), 0.0), axis=1, keepdims=True
    )
    holder = jnp.where(flag == 0.0, placed, jnp.where(placed >= 64.0, placed - 64.0, placed + 64.0))
    offset = lane & (PLANE - 1)
    spot = ((((offset >> 2) + y) & (NY - 1)) * NZ + z) * NX + ((offset + x) & (NX - 1))
    where_to = jnp.where((holder == spot.astype(F32)) & (lane < 2 * PLANE), 1.0, 0.0).astype(BF16)

    for copy in meta_copies:
        copy.wait_recv()
    info = meta[...].reshape(NZ * ROWS, 128)
    named = jnp.zeros((128, 128), F32)
    weight = jnp.zeros((128, 128), F32)
    for k in range(8):
        hit = info[:, k:k + 1] == lane_f
        named = named + jnp.where(hit, 1.0, 0.0)
        weight = weight + jnp.where(hit, info[:, 8 + k:9 + k], 0.0)
    at = dot(named.astype(BF16), where_to)
    before = jnp.where(((line >> 4) == (lane >> 4)) & (lane < line), 1.0, 0.0).astype(BF16)
    rank = dot(before, at.astype(BF16))
    pick = jnp.where(rank == (lane >> 4).astype(F32), at, 0.0)
    high = weight.astype(BF16)
    low = (weight - high.astype(F32)).astype(BF16)
    tables = (pick.T, (dot(high, where_to) * pick).T, (dot(low, where_to) * pick).T)
    own = lax.broadcasted_iota(jnp.int32, (NZ, 128), 0) == (lax.broadcasted_iota(jnp.int32, (NZ, 128), 1) >> 4)
    for r in range(2):
        for t, table in enumerate(tables):
            spread = jnp.where(own[None], table[r * PLANE:(r + 1) * PLANE][:, None, :], 0.0)
            if t == 0:
                sel[:, r] = spread
            else:
                comb[t - 1, :, r] = spread
    chosen = sel[...].reshape(256, 128).astype(BF16)
    for t in range(2):
        flat = comb[t].reshape(256, 128)
        comb_t[pl.ds(t * 128, 128), 0:128] = flat[0:128].T.astype(BF16)
        comb_t[pl.ds(t * 128, 128), 128:256] = flat[128:256].T.astype(BF16)

    for s in range(1, 4):
        for c in range(CHUNKS):
            for way in ag_steps(c):
                if s < len(way):
                    started[(c, way[s - 1][1])].wait_recv()
                    ag_start(c, *way[s])

    def go(c, d):
        return remote(away.at[c, d], rows.at[c, 0, d], go_send.at[c], go_recv.at[c], in_plane(d % NX, d // NX))

    def go_all(c):
        return remote(away.at[c, pl.ds(1, PLANE - 1)], rows.at[c, 0, pl.ds(1, PLANE - 1)], go_send.at[c], go_recv.at[c], sibling)

    for c in range(CHUNKS):
        for way in ag_steps(c):
            started[(c, way[-1][1])].wait_recv()
            if len(way) == 3:
                pass
        block = tok[c].reshape(NZ * ROWS, CW)
        for n in range(0, CW, TILE):
            piece = dot(chosen, block[:, n:n + TILE]).astype(BF16).reshape(PLANE, ROWS, TILE)
            away[c, :, :, n:n + TILE] = piece
        rows[c, 0, 0] = away[c, 0]
        for d in range(1, PLANE):
            go(c, d).start()

    for load in loads[:2]:
        load.wait()

    def share(c):
        return remote(rows.at[c, 0], rows.at[c, 1], sib_send.at[c], sib_recv.at[c], sibling)

    def first(c, side):
        block = rows[c, side].reshape(256, CW)
        for n in range(0, 2 * HALF, TILE):
            term = dot(block, w_in[c * CW:(c + 1) * CW, n:n + TILE])
            at_rows = pl.ds(side * 256, 256)
            if c == 0:
                acc[at_rows, n:n + TILE] = term
            else:
                acc[at_rows, n:n + TILE] += term

    for c in range(CHUNKS):
        go_all(c).wait_recv()
        share(c).start()
        first(c, 0)
        if c > 0:
            share(c - 1).wait_recv()
            first(c - 1, 1)
    share(CHUNKS - 1).wait_recv()
    first(CHUNKS - 1, 1)

    gate_act = acc[:, 0:HALF]
    hid[...] = (gate_act / (1.0 + jnp.exp(-gate_act)) * acc[:, HALF:2 * HALF]).astype(BF16)
    loads[2].wait()

    def pair(c):
        return remote(theirs.at[c], got.at[c], half_send.at[c], half_recv.at[c], sibling)

    for c in range(CHUNKS):
        for n in range(0, CW, TILE):
            theirs[c, :, n:n + TILE] = dot(hid[256:512], w_out[:, c * CW + n:c * CW + n + TILE]).astype(BF16)
        pair(c).start()
        for n in range(0, CW, TILE):
            mine[c, :, n:n + TILE] = dot(hid[0:256], w_out[:, c * CW + n:c * CW + n + TILE]).astype(BF16)

    def home(c, d):
        return remote(ret.at[c, d], back.at[c, d], back_send.at[c], back_recv.at[c], in_plane(-(d % NX), -(d // NX)))

    def home_all(c):
        return remote(ret.at[c, pl.ds(1, PLANE - 1)], back.at[c, pl.ds(1, PLANE - 1)], back_send.at[c], back_recv.at[c], sibling)

    for c in range(CHUNKS):
        pair(c).wait_recv()
        both = (mine[c].astype(F32) + got[c].astype(F32)).astype(BF16)
        ret[c] = both.reshape(PLANE, ROWS, CW)
        back[c, 0] = ret[c, 0]
        for d in range(1, PLANE):
            home(c, d).start()

    def rs_steps(c):
        up, down = (4, 4 + 1) if c % 2 == 0 else (3, 4)
        return [(i, i - 1) for i in range(up, 0, -1)], [(i, i + 1) for i in range(down, NZ)]

    def rs(c, src, dst):
        by = 1 if dst < src else -1
        return remote(hop_out.at[c, src], hop_in.at[c, dst], rs_send.at[c, src], rs_recv.at[c, dst], along_z(by))

    for tick in range(CHUNKS + 4):
        if tick < CHUNKS:
            c = tick
            home_all(c).wait_recv()
            block = back[c].reshape(256, CW)
            for n in range(0, CW, TILE):
                two = dot(comb_t[...], block[:, n:n + TILE])
                part[c, :, :, n:n + TILE] = (two[0:128] + two[128:256]).reshape(NZ, ROWS, TILE)
            for way in rs_steps(c):
                src, dst = way[0]
                hop_out[c, src] = part[c, src].astype(BF16)
                rs(c, src, dst).start()
        for c in range(max(0, tick - 4), min(tick, CHUNKS)):
            step = tick - c
            for way in rs_steps(c):
                if step < len(way):
                    src, dst = way[step]
                    rs(c, *way[step - 1]).wait_recv()
                    hop_out[c, src] = (part[c, src] + hop_in[c, src].astype(F32)).astype(BF16)
                    rs(c, src, dst).start()
                elif step == len(way):
                    rs(c, *way[step - 1]).wait_recv()
            if step == 4:
                total = part[c, 0] + hop_in[c, 0].astype(F32) + hop_in[c, NZ].astype(F32)
                out[:, c * CW:(c + 1) * CW] = total.astype(BF16)

    for copy in meta_copies:
        copy.wait_send()
    for copy in started.values():
        copy.wait_send()
    for c in range(CHUNKS):
        go_all(c).wait_send()
        share(c).wait_send()
        pair(c).wait_send()
        home_all(c).wait_send()
        for way in rs_steps(c):
            for step in way:
                rs(c, *step).wait_send()


def on_device(tokens, routes, route_gates, placement, swap_flags, gate_weight, up_weight, down_weight):
    vmem = pl.BlockSpec(memory_space=pltpu.VMEM)
    hbm = pl.BlockSpec(memory_space=pl.ANY)
    dma = pltpu.SemaphoreType.DMA
    return pl.pallas_call(
        kernel,
        out_shape=jax.ShapeDtypeStruct(tokens.shape, tokens.dtype),
        in_specs=[vmem] * 5 + [hbm] * 3,
        out_specs=vmem,
        scratch_shapes=[
            pltpu.VMEM((CHUNKS, NZ, ROWS, CW), BF16),
            pltpu.VMEM((NZ, ROWS, 128), F32),
            pltpu.VMEM((PLANE, 2, NZ, 128), F32),
            pltpu.VMEM((2, PLANE, 2, NZ, 128), F32),
            pltpu.VMEM((256, 256), BF16),
            pltpu.VMEM((CHUNKS, PLANE, ROWS, CW), BF16),
            pltpu.VMEM((CHUNKS, 2, PLANE, ROWS, CW), BF16),
            pltpu.VMEM((WIDE, 2 * HALF), BF16),
            pltpu.VMEM((HALF, WIDE), BF16),
            pltpu.VMEM((512, 2 * HALF), F32),
            pltpu.VMEM((512, HALF), BF16),
            pltpu.VMEM((CHUNKS, 256, CW), BF16),
            pltpu.VMEM((CHUNKS, 256, CW), BF16),
            pltpu.VMEM((CHUNKS, 256, CW), BF16),
            pltpu.VMEM((CHUNKS, PLANE, ROWS, CW), BF16),
            pltpu.VMEM((CHUNKS, PLANE, ROWS, CW), BF16),
            pltpu.VMEM((CHUNKS, NZ, ROWS, CW), F32),
            pltpu.VMEM((CHUNKS, NZ, ROWS, CW), BF16),
            pltpu.VMEM((CHUNKS, NZ + 1, ROWS, CW), BF16),
            dma((3,)),
            dma((NZ,)), dma((NZ,)),
            dma((CHUNKS, NZ)), dma((CHUNKS, NZ)),
            dma((CHUNKS,)), dma((CHUNKS,)),
            dma((CHUNKS,)), dma((CHUNKS,)),
            dma((CHUNKS,)), dma((CHUNKS,)),
            dma((CHUNKS,)), dma((CHUNKS,)),
            dma((CHUNKS, NZ)), dma((CHUNKS, NZ + 1)),
        ],
        compiler_params=pltpu.CompilerParams(
            collective_id=0, has_side_effects=True, vmem_limit_bytes=60 * 2**20
        ),
        name="moe",
    )(
        tokens, routes, route_gates, placement.reshape(1, -1), swap_flags.reshape(1, -1),
        gate_weight, up_weight, down_weight,
    )


def solution(mesh):
    return jax.shard_map(
        on_device,
        mesh=mesh,
        in_specs=(
            P(("dp", "expert"), None),
            P(("dp", "expert"), None),
            P(("dp", "expert"), None),
            P(),
            P(),
            P("expert", None, "dp"),
            P("expert", None, "dp"),
            P("expert", "dp", None),
        ),
        out_specs=P(("dp", "expert"), None),
        check_vma=False,
    )
```

time: 530 us -> 103 us (0.19)
  waiting for transfers between devices: 312 us -> 0 us
  blocking collectives: 109 us -> 0 us
  Pallas kernels: 0 us -> 98.7 us
  local copies, waits for them, and re-layouts: 55.8 us -> 4.27 us
  starting transfers between devices: 24.6 us -> 0 us
  matrix products: 22.4 us -> 0 us
    all_to_all x2 -> x0, waiting for transfers between devices: 182 us -> none  [the longest x1 96.3 us: on_device(): lax.all_to_all(lax.all_to_all(partial_value, 'dp', split_axis=0, concat_a...]
    ppermute x3 -> x0, waiting for transfers between devices: 130 us -> none  [passed_along(): lax.ppermute(value, axis, [(i, (i + by) % peers) for i in range(peers)])]
    all_to_all x2 -> x0, blocking collectives: 109 us -> none  [the longest x1 54.7 us: on_device(): lax.all_to_all(doubled, 'dp', split_axis=0, concat_axis=0, tiled=True)]
    pallas_call x0 -> x1, Pallas kernels: none -> 98.7 us  [on_device(): pl.pallas_call(kernel, out_shape=jax.ShapeDtypeStruct(tokens.shape, token...]
    dot_general x7 -> x0, matrix products: 22.4 us -> none  [the longest x1 6.39 us: expert_block(): up_act = jnp.dot(received, w_up, preferred_element_type=jnp.float32)]
    all_to_all x3 -> x0, local copies, waits for them, and re-layouts: 22.2 us -> none  [the longest x1 9.95 us: on_device(): lax.all_to_all(lax.all_to_all(doubled, 'dp', split_axis=0, concat_axis=0,...]
    reshape x3 -> x0, local copies, waits for them, and re-layouts: 18 us -> none  [the longest x1 7.67 us: on_device(): partial_value = partial_value.reshape(replicas, columns, capacity, features)]
    all_to_all x2 -> x0, starting transfers between devices: 17.8 us -> none  [the longest x1 10.7 us: on_device(): lax.all_to_all(lax.all_to_all(doubled, 'dp', split_axis=0, concat_axis=0,...]
  transfers between devices with their start and end apart: 5 -> 0, of which waited for: 5 -> 0; matrix products, arithmetic and copies ran while one was open for 5% -> 0% of each run, Pallas kernels for 0% -> 0%
where the time goes in v1:
time: 103 us
  Pallas kernels  98.7 us (96%)
  local copies, waits for them, and re-layouts  4.27 us (4%)
    pallas_call x1, Pallas kernels, on_device(): pl.pallas_call(kernel, out_shape=jax.ShapeDtypeStruct(tokens.shape, token...  98.7 us
    unnamed x3, local copies, waits for them, and re-layouts  4.27 us

profile of v1, /device:TPU:2, one launch (start us, length us, event | category | flops | bytes accessed | tf_op | source)
XLA Modules:
  0.0 103.0 jit_solution(4811533417159504503)
XLA Ops:
  0.0 1.4 %copy.9.routes = s32[16,8]{1,0:T(8,128)} copy(s32[16,8]{0,1:T(8,128)} %param.9) | data formatting | bytes 1024 | tf_op args[1]
  1.4 1.4 %copy.10.gates = f32[16,8]{1,0:T(8,128)} copy(f32[16,8]{0,1:T(8,128)} %param.10) | data formatting | bytes 1024 | tf_op args[2]
  2.7 98.7 %moe.1 = bf16[16,4096]{1,0:T(8,128)(2,1)} custom-call(bf16[16,4096]{1,0:T(8,128)(2,1)} %tokens.1, s32[16,8]{1,0:T(8,128)} %copy.9.routes, f32[16,8]{1,0:T(8,128)} %copy.10.gates, s32[1,128]{1,0:T(1,128)} %bitcast.2, s32[1,128]{1,0:T(1,128)} %bitcast.3, bf16[1,4096,384]{2,1,0:T(8,128)(2,1)} %w_gate.1, bf16[1,4096,384]{2,1,0:T(8,128)(2,1)} %w_up.1, ...), custom_call_target="tpu_custom_call" | custom-call | tf_op jit(solution)/shard_map/moe/pallas_call | solution.py:272
  101.4 1.6 %copy.12 = bf16[16,4096]{1,0:T(8,128)(2,1)} copy(bf16[16,4096]{1,0:T(8,128)(2,1)} %moe.1) | data formatting | bytes 262144

commit v2 on v0

v2 whole, which is shorter than its diff:
```python
import jax
import jax.numpy as jnp
from jax import lax
from jax.experimental import pallas as pl
from jax.experimental.pallas import tpu as pltpu
from jax.sharding import PartitionSpec as P

NX, NY, NZ = 4, 4, 8
OFFSETS = (
    (0, 0), (1, 0), (3, 0), (0, 1), (0, 3), (2, 0), (0, 2), (2, 2),
    (1, 1), (3, 3), (1, 3), (3, 1), (1, 2), (3, 2), (2, 1), (2, 3),
)
PLANE = len(OFFSETS)
GROUPS = 2
PEERS = PLANE // GROUPS
ROWS = 16
WIDE = 4096
HALF = 384
TILE = 256
GO_WIDTHS = (512, 1024, 1024, 1024, 512)
BACK_WIDTHS = (512, 1024, 1024, 1024, 512)
MESH = pl.DeviceIdType.MESH
F32 = jnp.float32
BF16 = jnp.bfloat16


def spans(widths):
    starts = [sum(widths[:c]) for c in range(len(widths))]
    return list(zip(starts, widths))


GO = spans(GO_WIDTHS)
BACK = spans(BACK_WIDTHS)


def dot(a, b):
    return jnp.dot(a, b, preferred_element_type=F32)


def kernel(
    tokens, routes, gates, placement, flags, w_gate, w_up, w_down, out,
    tok, turned, meta, sel, comb, comb_t, away, rows, w_in, w_out, acc, hid,
    mine, theirs, got, ret, back, part, hop_out, hop_in,
    w_sem, meta_send, meta_recv, ag_send, ag_recv, go_send, go_recv, sib_send, sib_recv,
    half_send, half_recv, back_send, back_recv, rs_send, rs_recv,
):
    dp = lax.axis_index("dp")
    ex = lax.axis_index("expert")
    x, core = dp // 2, dp % 2
    y, z = ex // NZ, ex % NZ
    sibling = (x * 2 + (1 - core), ex)

    def along_z(by):
        return (dp, y * NZ + (z + by + NZ) % NZ)

    def in_plane(d, sign):
        dx, dy = OFFSETS[d]
        return (((x + sign * dx + NX) % NX) * 2 + core, ((y + sign * dy + NY) % NY) * NZ + z)

    def remote(src, dst, send, recv, device):
        return pltpu.make_async_remote_copy(
            src_ref=src, dst_ref=dst, send_sem=send, recv_sem=recv, device_id=device, device_id_type=MESH
        )

    barrier = pltpu.get_barrier_semaphore()
    for i in range(1, NZ):
        pl.semaphore_signal(barrier, inc=1, device_id=along_z(i), device_id_type=MESH)
    for d in range(1, PLANE):
        pl.semaphore_signal(barrier, inc=1, device_id=in_plane(d, 1), device_id_type=MESH)
    pl.semaphore_signal(barrier, inc=1, device_id=sibling, device_id_type=MESH)

    loads = (
        pltpu.make_async_copy(w_gate.at[0], w_in.at[:, pl.ds(0, HALF)], w_sem.at[0]),
        pltpu.make_async_copy(w_up.at[0], w_in.at[:, pl.ds(HALF, HALF)], w_sem.at[1]),
        pltpu.make_async_copy(w_down.at[0], w_out, w_sem.at[2]),
    )
    for load in loads:
        load.start()

    tok[0] = tokens[...]
    turned[...] = jnp.zeros((128, 128), F32)
    turned[0:8, 0:ROWS] = routes[...].astype(F32)
    turned[8:16, 0:ROWS] = gates[...]
    meta[0] = turned[...].T[0:ROWS]

    lane = lax.broadcasted_iota(jnp.int32, (128, 128), 1)
    line = lax.broadcasted_iota(jnp.int32, (128, 128), 0)
    lane_f = lane.astype(F32)
    placed = jnp.broadcast_to(placement[...].astype(F32), (128, 128)).T
    flag = jnp.sum(
        jnp.where(placed == lane_f, jnp.broadcast_to(flags[...].astype(F32), (128, 128)), 0.0), axis=1, keepdims=True
    )
    holder = jnp.where(flag == 0.0, placed, jnp.where(placed >= 64.0, placed - 64.0, placed + 64.0))
    slot = lax.broadcasted_iota(jnp.int32, (8, 128), 1)
    far_x = jnp.zeros((8, 128), jnp.int32)
    far_y = jnp.zeros((8, 128), jnp.int32)
    for d, (dx, dy) in enumerate(OFFSETS):
        here = (slot & (PLANE - 1)) == d
        far_x = jnp.where(here, dx, far_x)
        far_y = jnp.where(here, dy, far_y)
    spot = (((far_y + y) & (NY - 1)) * NZ + z) * NX + ((far_x + x) & (NX - 1))
    spot = jnp.where(slot < 2 * PLANE, spot, -1).astype(F32)[0:1]
    where_to = jnp.where(holder == spot, 1.0, 0.0).astype(BF16)

    pl.semaphore_wait(barrier, NZ - 1 + PLANE - 1 + 1)

    meta_copies = [
        remote(meta.at[0], meta.at[i], meta_send.at[i], meta_recv.at[i], along_z(-i)) for i in range(1, NZ)
    ]
    gather = {}

    def ag(c, src, dst, by):
        cols = pl.ds(*GO[c])
        gather[(c, dst)] = remote(
            tok.at[src, :, cols], tok.at[dst, :, cols], ag_send.at[c, dst], ag_recv.at[c, dst], along_z(by)
        )
        gather[(c, dst)].start()

    for c in range(len(GO)):
        for i in (4, 3, 5, 2, 6, 1, 7):
            ag(c, 0, i, -i)
        if c == 0:
            for copy in meta_copies:
                copy.start()

    for copy in meta_copies:
        copy.wait_recv()
    info = meta[...].reshape(NZ * ROWS, 128)
    named = jnp.zeros((128, 128), F32)
    weight = jnp.zeros((128, 128), F32)
    for k in range(8):
        hit = info[:, k:k + 1] == lane_f
        named = named + jnp.where(hit, 1.0, 0.0)
        weight = weight + jnp.where(hit, info[:, 8 + k:9 + k], 0.0)
    at = dot(named.astype(BF16), where_to)
    before = jnp.where(((line >> 4) == (lane >> 4)) & (lane < line), 1.0, 0.0).astype(BF16)
    rank = dot(before, at.astype(BF16))
    pick = jnp.where(rank == (lane >> 4).astype(F32), at, 0.0)
    own = lax.broadcasted_iota(jnp.int32, (NZ, 128), 0) == (lax.broadcasted_iota(jnp.int32, (NZ, 128), 1) >> 4)

    def spread(table, r):
        return jnp.where(own[None], table[r * PLANE:(r + 1) * PLANE][:, None, :], 0.0)

    picked = pick.T
    for r in range(2):
        sel[:, r] = spread(picked, r)
    chosen = sel[...].reshape(256, 128).astype(BF16)

    def go(g, c, p):
        cols = pl.ds(*GO[c])
        return remote(
            away.at[g, p, :, cols], rows.at[g, 0, p, :, cols], go_send.at[g, c], go_recv.at[g, c], in_plane(g * PEERS + p, 1)
        )

    def all_but_self(g):
        return pl.ds(1, PEERS - 1) if g == 0 else pl.ds(0, PEERS)

    def go_all(g, c):
        cols = pl.ds(*GO[c])
        return remote(
            away.at[g, all_but_self(g), :, cols], rows.at[g, 0, all_but_self(g), :, cols],
            go_send.at[g, c], go_recv.at[g, c], sibling,
        )

    def go_out(g, c):
        for p in range(1 - g, PEERS):
            go(g, c, p).start()

    last_go = len(GO) - 1
    for c, (start, width) in enumerate(GO):
        for i in range(1, NZ):
            gather[(c, i)].wait_recv()
        for n in range(start, start + width, TILE):
            block = tok[:, :, n:n + TILE].reshape(NZ * ROWS, TILE)
            piece = dot(chosen, block).astype(BF16).reshape(GROUPS, PEERS, ROWS, TILE)
            away[:, :, :, n:n + TILE] = piece
            rows[0, 0, 0, :, n:n + TILE] = piece[0, 0]
        go_out(0, c)
        go_out(1, c)

    high = weight.astype(BF16)
    low = (weight - high.astype(F32)).astype(BF16)
    for t, share_of in enumerate((high, low)):
        table = (dot(share_of, where_to) * pick).T
        for r in range(2):
            comb[:, r] = spread(table, r)
        flat = comb[...].reshape(256, 128)
        for g in range(GROUPS):
            comb_t[g, t * 128:(t + 1) * 128] = flat[g * 128:(g + 1) * 128].T.astype(BF16)

    for load in loads[:2]:
        load.wait()

    def share(g, c):
        cols = pl.ds(*GO[c])
        return remote(rows.at[g, 0, :, :, cols], rows.at[g, 1, :, :, cols], sib_send.at[g, c], sib_recv.at[g, c], sibling)

    def first(g, c):
        start, width = GO[c]
        block = rows[g, :, :, :, start:start + width].reshape(2 * PEERS * ROWS, width)
        for n in range(0, 2 * HALF, TILE):
            term = dot(block, w_in[start:start + width, n:n + TILE])
            if c == 0:
                acc[g, :, n:n + TILE] = term
            else:
                acc[g, :, n:n + TILE] += term

    def pair(g, c):
        cols = pl.ds(*BACK[c])
        return remote(theirs.at[g, :, cols], got.at[g, :, cols], half_send.at[g, c], half_recv.at[g, c], sibling)

    def home(g, c, p):
        cols = pl.ds(*BACK[c])
        return remote(
            ret.at[g, p, :, cols], back.at[g, p, :, cols], back_send.at[g, c], back_recv.at[g, c], in_plane(g * PEERS + p, -1)
        )

    def home_all(g, c):
        cols = pl.ds(*BACK[c])
        return remote(
            ret.at[g, all_but_self(g), :, cols], back.at[g, all_but_self(g), :, cols],
            back_send.at[g, c], back_recv.at[g, c], sibling,
        )

    def finish(g, c):
        start, width = BACK[c]
        cols = slice(start, start + width)
        pair(g, c).wait_recv()
        both = (mine[g, :, cols].astype(F32) + got[g, :, cols].astype(F32)).astype(BF16).reshape(PEERS, ROWS, width)
        ret[g, :, :, cols] = both
        if g == 0:
            back[0, 0, :, cols] = both[0]
        for p in range(1 - g, PEERS):
            home(g, c, p).start()

    def arrived(g, c):
        go_all(g, c).wait_recv()
        share(g, c).start()
        if c > 0:
            share(g, c - 1).wait_recv()
            first(g, c - 1)
        if c == last_go:
            share(g, c).wait_recv()
            first(g, c)

    def activate(g):
        gate_act = acc[g, :, 0:HALF]
        hid[g] = (gate_act / (1.0 + jnp.exp(-gate_act)) * acc[g, :, HALF:2 * HALF]).astype(BF16)

    def second(g, c):
        start, width = BACK[c]
        for n in range(start, start + width, TILE):
            two = dot(hid[g], w_out[:, n:n + TILE]).astype(BF16)
            mine[g, :, n:n + TILE] = two[0:128]
            theirs[g, :, n:n + TILE] = two[128:256]
        pair(g, c).start()

    for c in range(len(GO)):
        arrived(0, c)
    activate(0)
    loads[2].wait()
    for c in range(len(BACK)):
        second(0, c)
        if c > 0:
            finish(0, c - 1)
    finish(0, len(BACK) - 1)
    for c in range(len(GO)):
        arrived(1, c)
    activate(1)
    for c in range(len(BACK)):
        second(1, c)
        if c > 0:
            finish(1, c - 1)
    finish(1, len(BACK) - 1)

    def gathered(g, c):
        start, width = BACK[c]
        home_all(g, c).wait_recv()
        for n in range(start, start + width, TILE):
            block = back[g, :, :, n:n + TILE].reshape(PEERS * ROWS, TILE)
            two = dot(comb_t[g], block)
            two = (two[0:128] + two[128:256]).reshape(NZ, ROWS, TILE)
            if g == 0:
                part[:, :, n:n + TILE] = two
            else:
                part[:, :, n:n + TILE] += two

    def rs(c, src, dst, by):
        cols = pl.ds(*BACK[c])
        return remote(
            hop_out.at[src, :, cols], hop_in.at[dst, :, cols], rs_send.at[c, src], rs_recv.at[c, dst], along_z(by)
        )

    last = len(BACK) - 1

    def rs_to_mid(c):
        if c == last:
            return ()
        return (rs(c, 3, 4, 1), rs(c, 5, 5, -1), rs(c, 4, 6, 2 if c % 2 == 0 else -2))

    def rs_near(c):
        if c == last:
            return tuple(rs(c, i, i - 1, i) for i in (4, 3, 5, 2, 6, 1, 7))
        return (rs(c, 1, 0, 1), rs(c, 7, 1, -1))

    def rs_second(c):
        if c == last:
            return ()
        return (rs(c, 2, 2, 2), rs(c, 6, 3, -2))

    def middle(c):
        start, width = BACK[c]
        cols = slice(start, start + width)
        for copy in rs_to_mid(c):
            copy.wait_recv()
        up = part[2, :, cols] + hop_in[4, :, cols].astype(F32)
        down = part[6, :, cols] + hop_in[5, :, cols].astype(F32)
        if c % 2 == 0:
            up = up + hop_in[6, :, cols].astype(F32)
        else:
            down = down + hop_in[6, :, cols].astype(F32)
        hop_out[2, :, cols] = up.astype(BF16)
        hop_out[6, :, cols] = down.astype(BF16)
        for copy in rs_second(c):
            copy.start()

    def done(c):
        start, width = BACK[c]
        cols = slice(start, start + width)
        for copy in rs_near(c) + rs_second(c):
            copy.wait_recv()
        total = part[0, :, cols]
        for i in range(NZ - 1 if c == last else 4):
            total = total + hop_in[i, :, cols].astype(F32)
        out[:, cols] = total.astype(BF16)

    for c in range(len(BACK)):
        gathered(0, c)

    for c in range(last + 1):
        start, width = BACK[c]
        cols = slice(start, start + width)
        gathered(1, c)
        for i in (4, 3, 5, 2, 6, 1, 7) if c == last else (4, 3, 5, 1, 7):
            hop_out[i, :, cols] = part[i, :, cols].astype(BF16)
        for copy in rs_to_mid(c) + rs_near(c):
            copy.start()
        if c > 0:
            middle(c - 1)
        if c > 1:
            done(c - 2)
    done(last - 1)
    done(last)

    for copy in meta_copies:
        copy.wait_send()
    for copy in gather.values():
        copy.wait_send()
    for g in range(GROUPS):
        for c in range(len(GO)):
            go_all(g, c).wait_send()
            share(g, c).wait_send()
        for c in range(len(BACK)):
            pair(g, c).wait_send()
            home_all(g, c).wait_send()
    for c in range(len(BACK)):
        for copy in rs_to_mid(c) + rs_near(c) + rs_second(c):
            copy.wait_send()


def on_device(tokens, routes, route_gates, placement, swap_flags, gate_weight, up_weight, down_weight):
    vmem = pl.BlockSpec(memory_space=pltpu.VMEM)
    hbm = pl.BlockSpec(memory_space=pl.ANY)
    dma = pltpu.SemaphoreType.DMA
    lanes = PEERS * ROWS
    n_go, n_back = len(GO), len(BACK)
    return pl.pallas_call(
        kernel,
        out_shape=jax.ShapeDtypeStruct(tokens.shape, tokens.dtype),
        in_specs=[vmem] * 5 + [hbm] * 3,
        out_specs=vmem,
        scratch_shapes=[
            pltpu.VMEM((NZ, ROWS, WIDE), BF16),
            pltpu.VMEM((128, 128), F32),
            pltpu.VMEM((NZ, ROWS, 128), F32),
            pltpu.VMEM((PLANE, 2, NZ, 128), F32),
            pltpu.VMEM((PLANE, 2, NZ, 128), F32),
            pltpu.VMEM((GROUPS, 256, lanes), BF16),
            pltpu.VMEM((GROUPS, PEERS, ROWS, WIDE), BF16),
            pltpu.VMEM((GROUPS, 2, PEERS, ROWS, WIDE), BF16),
            pltpu.VMEM((WIDE, 2 * HALF), BF16),
            pltpu.VMEM((HALF, WIDE), BF16),
            pltpu.VMEM((GROUPS, 2 * lanes, 2 * HALF), F32),
            pltpu.VMEM((GROUPS, 2 * lanes, HALF), BF16),
            pltpu.VMEM((GROUPS, lanes, WIDE), BF16),
            pltpu.VMEM((GROUPS, lanes, WIDE), BF16),
            pltpu.VMEM((GROUPS, lanes, WIDE), BF16),
            pltpu.VMEM((GROUPS, PEERS, ROWS, WIDE), BF16),
            pltpu.VMEM((GROUPS, PEERS, ROWS, WIDE), BF16),
            pltpu.VMEM((NZ, ROWS, WIDE), F32),
            pltpu.VMEM((NZ, ROWS, WIDE), BF16),
            pltpu.VMEM((NZ - 1, ROWS, WIDE), BF16),
            dma((3,)),
            dma((NZ,)), dma((NZ,)),
            dma((n_go, NZ)), dma((n_go, NZ)),
            dma((GROUPS, n_go)), dma((GROUPS, n_go)),
            dma((GROUPS, n_go)), dma((GROUPS, n_go)),
            dma((GROUPS, n_back)), dma((GROUPS, n_back)),
            dma((GROUPS, n_back)), dma((GROUPS, n_back)),
            dma((n_back, NZ)), dma((n_back, NZ - 1)),
        ],
        compiler_params=pltpu.CompilerParams(
            collective_id=0, has_side_effects=True, vmem_limit_bytes=60 * 2**20
        ),
        name="moe",
    )(
        tokens, routes.T, route_gates.T, placement.reshape(1, -1), swap_flags.reshape(1, -1),
        gate_weight, up_weight, down_weight,
    )


def solution(mesh):
    return jax.shard_map(
        on_device,
        mesh=mesh,
        in_specs=(
            P(("dp", "expert"), None),
            P(("dp", "expert"), None),
            P(("dp", "expert"), None),
            P(),
            P(),
            P("expert", None, "dp"),
            P("expert", None, "dp"),
            P("expert", "dp", None),
        ),
        out_specs=P(("dp", "expert"), None),
        check_vma=False,
    )
```

time: 530 us -> 89.7 us (0.17)
  waiting for transfers between devices: 312 us -> 0 us
  blocking collectives: 109 us -> 0 us
  Pallas kernels: 0 us -> 87.7 us
  local copies, waits for them, and re-layouts: 55.8 us -> 1.57 us
  starting transfers between devices: 24.6 us -> 0 us
  matrix products: 22.4 us -> 0 us
    all_to_all x2 -> x0, waiting for transfers between devices: 182 us -> none  [the longest x1 96.3 us: on_device(): lax.all_to_all(lax.all_to_all(partial_value, 'dp', split_axis=0, concat_a...]
    ppermute x3 -> x0, waiting for transfers between devices: 130 us -> none  [passed_along(): lax.ppermute(value, axis, [(i, (i + by) % peers) for i in range(peers)])]
    all_to_all x2 -> x0, blocking collectives: 109 us -> none  [the longest x1 54.7 us: on_device(): lax.all_to_all(doubled, 'dp', split_axis=0, concat_axis=0, tiled=True)]
    pallas_call x0 -> x1, Pallas kernels: none -> 87.7 us  [on_device(): pl.pallas_call(kernel, out_shape=jax.ShapeDtypeStruct(tokens.shape, token...]
    dot_general x7 -> x0, matrix products: 22.4 us -> none  [the longest x1 6.39 us: expert_block(): up_act = jnp.dot(received, w_up, preferred_element_type=jnp.float32)]
    all_to_all x3 -> x0, local copies, waits for them, and re-layouts: 22.2 us -> none  [the longest x1 9.95 us: on_device(): lax.all_to_all(lax.all_to_all(doubled, 'dp', split_axis=0, concat_axis=0,...]
    reshape x3 -> x0, local copies, waits for them, and re-layouts: 18 us -> none  [the longest x1 7.67 us: on_device(): partial_value = partial_value.reshape(replicas, columns, capacity, features)]
    all_to_all x2 -> x0, starting transfers between devices: 17.8 us -> none  [the longest x1 10.7 us: on_device(): lax.all_to_all(lax.all_to_all(doubled, 'dp', split_axis=0, concat_axis=0,...]
  transfers between devices with their start and end apart: 5 -> 0, of which waited for: 5 -> 0; matrix products, arithmetic and copies ran while one was open for 5% -> 0% of each run, Pallas kernels for 0% -> 0%
where the time goes in v2:
time: 89.7 us; the launch traced here: 89.2 us
  Pallas kernels  87.7 us (98%)
  local copies, waits for them, and re-layouts  1.57 us (2%)
    pallas_call x1, Pallas kernels, on_device(): pl.pallas_call(kernel, out_shape=jax.ShapeDtypeStruct(tokens.shape, token...  87.7 us

profile of v2, /device:TPU:2, one launch (start us, length us, event | category | flops | bytes accessed | tf_op | source)
XLA Modules:
  0.0 89.2 jit_solution(14340146028222495801)
XLA Ops:
  0.0 87.7 %moe.1 = bf16[16,4096]{1,0:T(8,128)(2,1)} custom-call(bf16[16,4096]{1,0:T(8,128)(2,1)} %tokens.1, s32[8,16]{1,0:T(8,128)} %bitcast.4, f32[8,16]{1,0:T(8,128)} %bitcast.5, s32[1,128]{1,0:T(1,128)} %bitcast.6, s32[1,128]{1,0:T(1,128)} %bitcast.7, bf16[1,4096,384]{2,1,0:T(8,128)(2,1)} %w_gate.1, bf16[1,4096,384]{2,1,0:T(8,128)(2,1)} %w_up.1, ...), custom_call_target="tpu_custom_call" | custom-call | tf_op jit(solution)/shard_map/moe/pallas_call | solution.py:377
  87.7 1.6 %copy.10 = bf16[16,4096]{1,0:T(8,128)(2,1)} copy(bf16[16,4096]{1,0:T(8,128)(2,1)} %moe.1) | data formatting | bytes 262144

commit v3 on v2

v3 whole, which is shorter than its diff:
```python
import jax
import jax.numpy as jnp
from jax import lax
from jax.experimental import pallas as pl
from jax.experimental.pallas import tpu as pltpu
from jax.sharding import PartitionSpec as P

NX, NY, NZ = 4, 4, 8
OFFSETS = (
    (0, 0), (1, 0), (3, 0), (0, 1), (0, 3), (2, 0), (0, 2), (2, 2),
    (1, 1), (3, 3), (1, 3), (3, 1), (1, 2), (3, 2), (2, 1), (2, 3),
)
PLANE = len(OFFSETS)
SOURCES = (0, 1, 2, 7, 3, 4, 5, 6)
GROUPS = 2
NEAR = NZ // GROUPS
ROWS = 16
SOME = 2 * NEAR
WIDE = 4096
HALF = 384
TILE = 256
GO_WIDTHS = ((512, 1536, 2048), (1024, 1024, 1024, 1024))
BACK_WIDTHS = ((1024, 3072), (1024, 1024, 1024, 512, 512))
MESH = pl.DeviceIdType.MESH
F32 = jnp.float32
BF16 = jnp.bfloat16


def spans(widths):
    starts = [sum(widths[:c]) for c in range(len(widths))]
    return list(zip(starts, widths))


GO = tuple(spans(widths) for widths in GO_WIDTHS)
BACK = tuple(spans(widths) for widths in BACK_WIDTHS)
MOST_GO = max(len(widths) for widths in GO)
MOST_BACK = max(len(widths) for widths in BACK)


def dot(a, b):
    return jnp.dot(a, b, preferred_element_type=F32)


def kernel(
    tokens, routes, gates, placement, flags, w_gate, w_up, w_down, out,
    tok, turned, meta, sel, comb_t, away, rows, w_in, w_out, acc, hid,
    mine, theirs, got, ret, back, part, hop_out, hop_in,
    w_sem, meta_send, meta_recv, ag_send, ag_recv, go_send, go_recv, sib_send, sib_recv,
    half_send, half_recv, back_send, back_recv, rs_send, rs_recv,
):
    dp = lax.axis_index("dp")
    ex = lax.axis_index("expert")
    x, core = dp // 2, dp % 2
    y, z = ex // NZ, ex % NZ
    sibling = (x * 2 + (1 - core), ex)

    def along_z(by):
        return (dp, y * NZ + (z + by * (1 - 2 * core) + NZ) % NZ)

    def in_plane(d, sign):
        dx, dy = OFFSETS[d]
        return (((x + sign * dx + NX) % NX) * 2 + core, ((y + sign * dy + NY) % NY) * NZ + z)

    def remote(src, dst, send, recv, device):
        return pltpu.make_async_remote_copy(
            src_ref=src, dst_ref=dst, send_sem=send, recv_sem=recv, device_id=device, device_id_type=MESH
        )

    barrier = pltpu.get_barrier_semaphore()
    for i in range(1, NZ):
        pl.semaphore_signal(barrier, inc=1, device_id=along_z(i), device_id_type=MESH)
    for d in range(1, PLANE):
        pl.semaphore_signal(barrier, inc=1, device_id=in_plane(d, 1), device_id_type=MESH)
    pl.semaphore_signal(barrier, inc=1, device_id=sibling, device_id_type=MESH)

    loads = (
        pltpu.make_async_copy(w_gate.at[0], w_in.at[:, pl.ds(0, HALF)], w_sem.at[0]),
        pltpu.make_async_copy(w_up.at[0], w_in.at[:, pl.ds(HALF, HALF)], w_sem.at[1]),
        pltpu.make_async_copy(w_down.at[0], w_out, w_sem.at[2]),
    )
    for load in loads:
        load.start()

    tok[0] = tokens[...]
    turned[...] = jnp.zeros((128, 128), F32)
    turned[0:8, 0:ROWS] = routes[...].astype(F32)
    turned[8:16, 0:ROWS] = gates[...]
    meta[0] = turned[...].T[0:ROWS]

    lane = lax.broadcasted_iota(jnp.int32, (128, 128), 1)
    line = lax.broadcasted_iota(jnp.int32, (128, 128), 0)
    lane_f = lane.astype(F32)
    placed = jnp.broadcast_to(placement[...].astype(F32), (128, 128)).T
    flag = jnp.sum(
        jnp.where(placed == lane_f, jnp.broadcast_to(flags[...].astype(F32), (128, 128)), 0.0), axis=1, keepdims=True
    )
    holder = jnp.where(flag == 0.0, placed, jnp.where(placed >= 64.0, placed - 64.0, placed + 64.0))
    slot = lax.broadcasted_iota(jnp.int32, (8, 128), 1)
    far_x = jnp.zeros((8, 128), jnp.int32)
    far_y = jnp.zeros((8, 128), jnp.int32)
    for d, (dx, dy) in enumerate(OFFSETS):
        here = (slot & (PLANE - 1)) == d
        far_x = jnp.where(here, dx, far_x)
        far_y = jnp.where(here, dy, far_y)
    spot = (((far_y + y) & (NY - 1)) * NZ + z) * NX + ((far_x + x) & (NX - 1))
    spot = jnp.where(slot < 2 * PLANE, spot, -1).astype(F32)[0:1]
    where_to = jnp.where(holder == spot, 1.0, 0.0).astype(BF16)

    pl.semaphore_wait(barrier, NZ - 1 + PLANE - 1 + 1)

    meta_copies = [
        remote(meta.at[0], meta.at[q], meta_send.at[q], meta_recv.at[q], along_z(-SOURCES[q])) for q in range(1, NZ)
    ]
    gather = {}

    def ag(g, c, q):
        cols = pl.ds(*GO[g][c])
        gather[(g, c, q)] = remote(
            tok.at[0, :, cols], tok.at[q, :, cols], ag_send.at[c, q], ag_recv.at[c, q], along_z(-SOURCES[q])
        )
        gather[(g, c, q)].start()

    def slots(g):
        return (2, 1, 3) if g == 0 else (5, 4, 6, 7)

    for g in range(GROUPS):
        for c in range(len(GO[g])):
            for q in slots(g):
                ag(g, c, q)
            if g == 0 and c == 0:
                for copy in meta_copies:
                    copy.start()

    for copy in meta_copies:
        copy.wait_recv()
    info = meta[...].reshape(NZ * ROWS, 128)
    named = jnp.zeros((128, 128), F32)
    weight = jnp.zeros((128, 128), F32)
    for k in range(8):
        hit = info[:, k:k + 1] == lane_f
        named = named + jnp.where(hit, 1.0, 0.0)
        weight = weight + jnp.where(hit, info[:, 8 + k:9 + k], 0.0)
    at = dot(named.astype(BF16), where_to)
    before = jnp.where(((line >> 4) == (lane >> 4)) & (lane < line), 1.0, 0.0).astype(BF16)
    rank = dot(before, at.astype(BF16))
    pick = jnp.where(rank == (lane >> 4).astype(F32), at, 0.0)
    spot_row = lax.broadcasted_iota(jnp.int32, (SOME, 128), 0)
    spot_slot = lax.broadcasted_iota(jnp.int32, (SOME, 128), 1) >> 4
    second_rank = spot_row >= NEAR

    def spread(table, g):
        ours = spot_slot == (spot_row & (NEAR - 1)) + g * NEAR
        both = jnp.where(second_rank[None], table[PLANE:2 * PLANE][:, None, :], table[0:PLANE][:, None, :])
        sel[...] = jnp.where(ours[None], both, 0.0)
        return sel[...].reshape(PLANE * SOME, 128).T[g * 64:(g + 1) * 64]

    picked = pick.T
    chosen = [spread(picked, g).T.astype(BF16) for g in range(GROUPS)]

    def go(g, c, p):
        cols = pl.ds(*GO[g][c])
        return remote(
            away.at[g, p, :, cols], rows.at[g, 0, p, :, cols], go_send.at[g, c], go_recv.at[g, c], in_plane(p, 1)
        )

    others = pl.ds(1, PLANE - 1)

    def go_all(g, c):
        cols = pl.ds(*GO[g][c])
        return remote(
            away.at[g, others, :, cols], rows.at[g, 0, others, :, cols], go_send.at[g, c], go_recv.at[g, c], sibling
        )

    def dispatch(g, c):
        start, width = GO[g][c]
        for q in slots(g):
            gather[(g, c, q)].wait_recv()
        for n in range(start, start + width, TILE):
            block = tok[g * NEAR:(g + 1) * NEAR, :, n:n + TILE].reshape(NEAR * ROWS, TILE)
            piece = dot(chosen[g], block).astype(BF16).reshape(PLANE, SOME, TILE)
            away[g, :, :, n:n + TILE] = piece
            rows[g, 0, 0, :, n:n + TILE] = piece[0]
        for p in range(1, PLANE):
            go(g, c, p).start()

    for c in range(len(GO[0])):
        dispatch(0, c)
    dispatch(1, 0)

    high = weight.astype(BF16)
    low = (weight - high.astype(F32)).astype(BF16)
    for t, share_of in enumerate((high, low)):
        table = (dot(share_of, where_to) * pick).T
        for g in range(GROUPS):
            comb_t[g, t * 64:(t + 1) * 64] = spread(table, g).astype(BF16)

    dispatch(1, 1)
    for load in loads:
        load.wait()

    def share(g, c):
        cols = pl.ds(*GO[g][c])
        return remote(rows.at[g, 0, :, :, cols], rows.at[g, 1, :, :, cols], sib_send.at[g, c], sib_recv.at[g, c], sibling)

    def first(g, c):
        start, width = GO[g][c]
        block = rows[g, :, :, :, start:start + width].reshape(2 * PLANE * SOME, width)
        for n in range(0, 2 * HALF, TILE):
            term = dot(block, w_in[start:start + width, n:n + TILE])
            if c == 0:
                acc[g, :, n:n + TILE] = term
            else:
                acc[g, :, n:n + TILE] += term

    def pair(g, c):
        cols = pl.ds(*BACK[g][c])
        return remote(theirs.at[g, :, cols], got.at[g, :, cols], half_send.at[g, c], half_recv.at[g, c], sibling)

    def home(g, c, p):
        cols = pl.ds(*BACK[g][c])
        return remote(
            ret.at[g, p, :, cols], back.at[g, p, :, cols], back_send.at[g, c], back_recv.at[g, c], in_plane(p, -1)
        )

    def home_all(g, c):
        cols = pl.ds(*BACK[g][c])
        return remote(
            ret.at[g, others, :, cols], back.at[g, others, :, cols], back_send.at[g, c], back_recv.at[g, c], sibling
        )

    def finish(g, c):
        start, width = BACK[g][c]
        cols = slice(start, start + width)
        pair(g, c).wait_recv()
        both = (mine[g, :, cols].astype(F32) + got[g, :, cols].astype(F32)).astype(BF16).reshape(PLANE, SOME, width)
        ret[g, :, :, cols] = both
        back[g, 0, :, cols] = both[0]
        for p in range(1, PLANE):
            home(g, c, p).start()

    def arrived(g, c):
        go_all(g, c).wait_recv()
        share(g, c).start()
        if c > 0:
            share(g, c - 1).wait_recv()
            first(g, c - 1)
        if c == len(GO[g]) - 1:
            share(g, c).wait_recv()
            first(g, c)

    def activate(g):
        gate_act = acc[g, :, 0:HALF]
        hid[g] = (gate_act / (1.0 + jnp.exp(-gate_act)) * acc[g, :, HALF:2 * HALF]).astype(BF16)

    def second(g, c):
        start, width = BACK[g][c]
        for n in range(start, start + width, TILE):
            two = dot(hid[g], w_out[:, n:n + TILE]).astype(BF16)
            mine[g, :, n:n + TILE] = two[0:128]
            theirs[g, :, n:n + TILE] = two[128:256]
        pair(g, c).start()

    def experts(g):
        activate(g)
        for c in range(len(BACK[g])):
            second(g, c)
            if c > 0:
                finish(g, c - 1)
        finish(g, len(BACK[g]) - 1)

    arrived(0, 0)
    dispatch(1, 2)
    arrived(0, 1)
    arrived(0, 2)
    dispatch(1, 3)
    experts(0)
    for c in range(len(GO[1])):
        arrived(1, c)
    experts(1)

    def gathered(g, c):
        start, width = BACK[g][c]
        home_all(g, c).wait_recv()
        for n in range(start, start + width, TILE):
            block = back[g, :, :, n:n + TILE].reshape(PLANE * SOME, TILE)
            two = dot(comb_t[g], block)
            part[g * NEAR:(g + 1) * NEAR, :, n:n + TILE] = (two[0:64] + two[64:128]).reshape(NEAR, ROWS, TILE)

    ends = BACK[1]
    last = len(ends) - 1
    slot_of = {far: q for q, far in enumerate(SOURCES)}

    def rs(c, far, dst, by):
        cols = pl.ds(*ends[c])
        return remote(
            hop_out.at[far, :, cols], hop_in.at[dst, :, cols], rs_send.at[c, far], rs_recv.at[c, dst], along_z(by)
        )

    def rs_near(c):
        return rs(c, 1, 0, 1), rs(c, 7, 1, -1)

    def rs_far(c):
        if c == last:
            return tuple(rs(c, far, dst, far) for far, dst in ((4, 4), (3, 5), (5, 6), (6, 3), (2, 2)))
        return rs(c, 3, 4, 1), rs(c, 5, 5, -1), rs(c, 4, 6, 2)

    def rs_second(c):
        return () if c == last else (rs(c, 2, 2, 2), rs(c, 6, 3, -2))

    def leave(c, fars):
        start, width = ends[c]
        cols = slice(start, start + width)
        for far in fars:
            hop_out[far, :, cols] = part[slot_of[far], :, cols].astype(BF16)

    def middle(c):
        start, width = ends[c]
        cols = slice(start, start + width)
        for copy in rs_far(c):
            copy.wait_recv()
        up = part[slot_of[2], :, cols] + hop_in[4, :, cols].astype(F32) + hop_in[6, :, cols].astype(F32)
        down = part[slot_of[6], :, cols] + hop_in[5, :, cols].astype(F32)
        hop_out[2, :, cols] = up.astype(BF16)
        hop_out[6, :, cols] = down.astype(BF16)
        for copy in rs_second(c):
            copy.start()

    def done(c):
        start, width = ends[c]
        cols = slice(start, start + width)
        for copy in rs_near(c) + (rs_far(c) if c == last else rs_second(c)):
            copy.wait_recv()
        total = part[0, :, cols]
        for i in range(NZ - 1 if c == last else 4):
            total = total + hop_in[i, :, cols].astype(F32)
        out[:, cols] = total.astype(BF16)

    for c in range(len(BACK[0])):
        gathered(0, c)
    for c in range(last + 1):
        leave(c, (1, 7))
        for copy in rs_near(c):
            copy.start()
    for c in range(last + 1):
        gathered(1, c)
        leave(c, (4, 3, 5, 6, 2) if c == last else (3, 5, 4))
        for copy in rs_far(c):
            copy.start()
        if c > 0:
            middle(c - 1)
        if c > 1:
            done(c - 2)
    done(last - 1)
    done(last)

    for copy in meta_copies:
        copy.wait_send()
    for copy in gather.values():
        copy.wait_send()
    for g in range(GROUPS):
        for c in range(len(GO[g])):
            go_all(g, c).wait_send()
            share(g, c).wait_send()
        for c in range(len(BACK[g])):
            pair(g, c).wait_send()
            home_all(g, c).wait_send()
    for c in range(last + 1):
        for copy in rs_near(c) + rs_far(c) + rs_second(c):
            copy.wait_send()


def on_device(tokens, routes, route_gates, placement, swap_flags, gate_weight, up_weight, down_weight):
    vmem = pl.BlockSpec(memory_space=pltpu.VMEM)
    hbm = pl.BlockSpec(memory_space=pl.ANY)
    dma = pltpu.SemaphoreType.DMA
    lanes = PLANE * SOME
    return pl.pallas_call(
        kernel,
        out_shape=jax.ShapeDtypeStruct(tokens.shape, tokens.dtype),
        in_specs=[vmem] * 5 + [hbm] * 3,
        out_specs=vmem,
        scratch_shapes=[
            pltpu.VMEM((NZ, ROWS, WIDE), BF16),
            pltpu.VMEM((128, 128), F32),
            pltpu.VMEM((NZ, ROWS, 128), F32),
            pltpu.VMEM((PLANE, SOME, 128), F32),
            pltpu.VMEM((GROUPS, 128, lanes), BF16),
            pltpu.VMEM((GROUPS, PLANE, SOME, WIDE), BF16),
            pltpu.VMEM((GROUPS, 2, PLANE, SOME, WIDE), BF16),
            pltpu.VMEM((WIDE, 2 * HALF), BF16),
            pltpu.VMEM((HALF, WIDE), BF16),
            pltpu.VMEM((GROUPS, 2 * lanes, 2 * HALF), F32),
            pltpu.VMEM((GROUPS, 2 * lanes, HALF), BF16),
            pltpu.VMEM((GROUPS, lanes, WIDE), BF16),
            pltpu.VMEM((GROUPS, lanes, WIDE), BF16),
            pltpu.VMEM((GROUPS, lanes, WIDE), BF16),
            pltpu.VMEM((GROUPS, PLANE, SOME, WIDE), BF16),
            pltpu.VMEM((GROUPS, PLANE, SOME, WIDE), BF16),
            pltpu.VMEM((NZ, ROWS, WIDE), F32),
            pltpu.VMEM((NZ, ROWS, WIDE), BF16),
            pltpu.VMEM((NZ - 1, ROWS, WIDE), BF16),
            dma((3,)),
            dma((NZ,)), dma((NZ,)),
            dma((MOST_GO, NZ)), dma((MOST_GO, NZ)),
            dma((GROUPS, MOST_GO)), dma((GROUPS, MOST_GO)),
            dma((GROUPS, MOST_GO)), dma((GROUPS, MOST_GO)),
            dma((GROUPS, MOST_BACK)), dma((GROUPS, MOST_BACK)),
            dma((GROUPS, MOST_BACK)), dma((GROUPS, MOST_BACK)),
            dma((MOST_BACK, NZ)), dma((MOST_BACK, NZ - 1)),
        ],
        compiler_params=pltpu.CompilerParams(
            collective_id=0, has_side_effects=True, vmem_limit_bytes=60 * 2**20
        ),
        name="moe",
    )(
        tokens, routes.T, route_gates.T, placement.reshape(1, -1), swap_flags.reshape(1, -1),
        gate_weight, up_weight, down_weight,
    )


def solution(mesh):
    return jax.shard_map(
        on_device,
        mesh=mesh,
        in_specs=(
            P(("dp", "expert"), None),
            P(("dp", "expert"), None),
            P(("dp", "expert"), None),
            P(),
            P(),
            P("expert", None, "dp"),
            P("expert", None, "dp"),
            P("expert", "dp", None),
        ),
        out_specs=P(("dp", "expert"), None),
        check_vma=False,
    )
```

time: 89.7 us -> 83.4 us (0.930)
  Pallas kernels: 87.7 us -> 81.7 us
    pallas_call x1, Pallas kernels: 87.7 us -> 81.7 us  [on_device(): pl.pallas_call(kernel, out_shape=jax.ShapeDtypeStruct(tokens.shape, token...]
where the time goes in v3:
time: 83.4 us; the launch traced here: 83.3 us
  Pallas kernels  81.7 us (98%)
  local copies, waits for them, and re-layouts  1.57 us (2%)
    pallas_call x1, Pallas kernels, on_device(): pl.pallas_call(kernel, out_shape=jax.ShapeDtypeStruct(tokens.shape, token...  81.7 us

profile of v3, /device:TPU:2, one launch (start us, length us, event | category | flops | bytes accessed | tf_op | source)
XLA Modules:
  0.0 83.3 jit_solution(17886005330371163912)
XLA Ops:
  0.0 81.7 %moe.1 = bf16[16,4096]{1,0:T(8,128)(2,1)} custom-call(bf16[16,4096]{1,0:T(8,128)(2,1)} %tokens.1, s32[8,16]{1,0:T(8,128)} %bitcast.4, f32[8,16]{1,0:T(8,128)} %bitcast.5, s32[1,128]{1,0:T(1,128)} %bitcast.6, s32[1,128]{1,0:T(1,128)} %bitcast.7, bf16[1,4096,384]{2,1,0:T(8,128)(2,1)} %w_gate.1, bf16[1,4096,384]{2,1,0:T(8,128)(2,1)} %w_up.1, ...), custom_call_target="tpu_custom_call" | custom-call | tf_op jit(solution)/shard_map/moe/pallas_call | solution.py:377
  81.7 1.6 %copy.10 = bf16[16,4096]{1,0:T(8,128)(2,1)} copy(bf16[16,4096]{1,0:T(8,128)(2,1)} %moe.1) | data formatting | bytes 262144

commit v4 on v3

--- a/solution.py
+++ b/solution.py
@@ -42,7 +42,8 @@
 
 
 def kernel(
-    tokens, routes, gates, placement, flags, w_gate, w_up, w_down, out,
+    tokens, routes_in, gates_in, placement_in, flags_in, w_gate, w_up, w_down, out,
+    routes, gates, placement, flags, summed, in_sem, out_sem,
     tok, turned, meta, sel, comb_t, away, rows, w_in, w_out, acc, hid,
     mine, theirs, got, ret, back, part, hop_out, hop_in,
     w_sem, meta_send, meta_recv, ag_send, ag_recv, go_send, go_recv, sib_send, sib_recv,
@@ -78,14 +79,49 @@
         pltpu.make_async_copy(w_up.at[0], w_in.at[:, pl.ds(HALF, HALF)], w_sem.at[1]),
         pltpu.make_async_copy(w_down.at[0], w_out, w_sem.at[2]),
     )
-    for load in loads:
+    small = (
+        pltpu.make_async_copy(routes_in, routes, in_sem.at[0]),
+        pltpu.make_async_copy(gates_in, gates, in_sem.at[1]),
+        pltpu.make_async_copy(placement_in, placement, in_sem.at[2]),
+        pltpu.make_async_copy(flags_in, flags, in_sem.at[3]),
+        pltpu.make_async_copy(tokens, tok.at[0], in_sem.at[4]),
+    )
+    for load in small + loads:
         load.start()
-
-    tok[0] = tokens[...]
+    for load in small:
+        load.wait()
+
     turned[...] = jnp.zeros((128, 128), F32)
     turned[0:8, 0:ROWS] = routes[...].astype(F32)
     turned[8:16, 0:ROWS] = gates[...]
     meta[0] = turned[...].T[0:ROWS]
+
+    pl.semaphore_wait(barrier, NZ - 1 + PLANE - 1 + 1)
+
+    meta_copies = [
+        remote(meta.at[0], meta.at[q], meta_send.at[q], meta_recv.at[q], along_z(-SOURCES[q])) for q in range(1, NZ)
+    ]
+    gather = {}
+
+    def ag(g, c, q, src, by):
+        cols = pl.ds(*GO[g][c])
+        gather[(g, c, q)] = remote(
+            src.at[:, cols], tok.at[q, :, cols], ag_send.at[c, q], ag_recv.at[c, q], along_z(by)
+        )
+        gather[(g, c, q)].start()
+
+    for c in range(len(GO[0])):
+        for q in (2, 1, 3):
+            ag(0, c, q, tok.at[0], -SOURCES[q])
+        if c == 0:
+            for copy in meta_copies:
+                copy.start()
+
+    def forward(c):
+        ag(1, c, 5, tok.at[2], -2)
+        ag(1, c, 6, tok.at[3], 2)
+        ag(1, c, 4, tok.at[2], -1)
+        ag(1, c, 7, tok.at[3], 1)
 
     lane = lax.broadcasted_iota(jnp.int32, (128, 128), 1)
     line = lax.broadcasted_iota(jnp.int32, (128, 128), 0)
@@ -106,31 +142,6 @@
     spot = jnp.where(slot < 2 * PLANE, spot, -1).astype(F32)[0:1]
     where_to = jnp.where(holder == spot, 1.0, 0.0).astype(BF16)
 
-    pl.semaphore_wait(barrier, NZ - 1 + PLANE - 1 + 1)
-
-    meta_copies = [
-        remote(meta.at[0], meta.at[q], meta_send.at[q], meta_recv.at[q], along_z(-SOURCES[q])) for q in range(1, NZ)
-    ]
-    gather = {}
-
-    def ag(g, c, q):
-        cols = pl.ds(*GO[g][c])
-        gather[(g, c, q)] = remote(
-            tok.at[0, :, cols], tok.at[q, :, cols], ag_send.at[c, q], ag_recv.at[c, q], along_z(-SOURCES[q])
-        )
-        gather[(g, c, q)].start()
-
-    def slots(g):
-        return (2, 1, 3) if g == 0 else (5, 4, 6, 7)
-
-    for g in range(GROUPS):
-        for c in range(len(GO[g])):
-            for q in slots(g):
-                ag(g, c, q)
-            if g == 0 and c == 0:
-                for copy in meta_copies:
-                    copy.start()
-
     for copy in meta_copies:
         copy.wait_recv()
     info = meta[...].reshape(NZ * ROWS, 128)
@@ -173,8 +184,12 @@
 
     def dispatch(g, c):
         start, width = GO[g][c]
-        for q in slots(g):
+        for q in range(max(1, g * NEAR), (g + 1) * NEAR):
             gather[(g, c, q)].wait_recv()
+        if g == 0:
+            for far in range(len(GO[1])):
+                if start < sum(GO[1][far]) <= start + width:
+                    forward(far)
         for n in range(start, start + width, TILE):
             block = tok[g * NEAR:(g + 1) * NEAR, :, n:n + TILE].reshape(NEAR * ROWS, TILE)
             piece = dot(chosen[g], block).astype(BF16).reshape(PLANE, SOME, TILE)
@@ -325,6 +340,10 @@
         for copy in rs_second(c):
             copy.start()
 
+    def written(c):
+        cols = pl.ds(*ends[c])
+        return pltpu.make_async_copy(summed.at[:, cols], out.at[:, cols], out_sem.at[c])
+
     def done(c):
         start, width = ends[c]
         cols = slice(start, start + width)
@@ -333,7 +352,8 @@
         total = part[0, :, cols]
         for i in range(NZ - 1 if c == last else 4):
             total = total + hop_in[i, :, cols].astype(F32)
-        out[:, cols] = total.astype(BF16)
+        summed[:, cols] = total.astype(BF16)
+        written(c).start()
 
     for c in range(len(BACK[0])):
         gathered(0, c)
@@ -367,19 +387,26 @@
     for c in range(last + 1):
         for copy in rs_near(c) + rs_far(c) + rs_second(c):
             copy.wait_send()
+        written(c).wait()
 
 
 def on_device(tokens, routes, route_gates, placement, swap_flags, gate_weight, up_weight, down_weight):
-    vmem = pl.BlockSpec(memory_space=pltpu.VMEM)
     hbm = pl.BlockSpec(memory_space=pl.ANY)
     dma = pltpu.SemaphoreType.DMA
     lanes = PLANE * SOME
     return pl.pallas_call(
         kernel,
         out_shape=jax.ShapeDtypeStruct(tokens.shape, tokens.dtype),
-        in_specs=[vmem] * 5 + [hbm] * 3,
-        out_specs=vmem,
+        in_specs=[hbm] * 8,
+        out_specs=hbm,
         scratch_shapes=[
+            pltpu.VMEM(routes.shape[::-1], jnp.int32),
+            pltpu.VMEM(route_gates.shape[::-1], F32),
+            pltpu.VMEM((1, 128), jnp.int32),
+            pltpu.VMEM((1, 128), jnp.int32),
+            pltpu.VMEM(tokens.shape, BF16),
+            dma((5,)),
+            dma((MOST_BACK,)),
             pltpu.VMEM((NZ, ROWS, WIDE), BF16),
             pltpu.VMEM((128, 128), F32),
             pltpu.VMEM((NZ, ROWS, 128), F32),

time: 83.4 us -> 79.4 us (0.952)
  Pallas kernels: 81.7 us -> 76.9 us
    pallas_call x1, Pallas kernels: 81.7 us -> 76.9 us  [on_device(): pl.pallas_call(kernel, out_shape=jax.ShapeDtypeStruct(tokens.shape, token...]
where the time goes in v4:
time: 79.4 us; the launch traced here: 78.5 us
  Pallas kernels  76.9 us (97%)
  local copies, waits for them, and re-layouts  1.57 us (2%)
    pallas_call x1, Pallas kernels, on_device(): pl.pallas_call(kernel, out_shape=jax.ShapeDtypeStruct(tokens.shape, token...  76.9 us

profile of v4, /device:TPU:2, one launch (start us, length us, event | category | flops | bytes accessed | tf_op | source)
XLA Modules:
  0.0 78.5 jit_solution(13053129377766083486)
XLA Ops:
  0.0 76.9 %moe.1 = bf16[16,4096]{1,0:T(8,128)(2,1)} custom-call(bf16[16,4096]{1,0:T(8,128)(2,1)} %tokens.1, s32[8,16]{1,0:T(8,128)} %bitcast.4, f32[8,16]{1,0:T(8,128)} %bitcast.5, s32[1,128]{1,0:T(1,128)} %bitcast.6, s32[1,128]{1,0:T(1,128)} %bitcast.7, bf16[1,4096,384]{2,1,0:T(8,128)(2,1)} %w_gate.1, bf16[1,4096,384]{2,1,0:T(8,128)(2,1)} %w_up.1, ...), custom_call_target="tpu_custom_call" | custom-call | tf_op jit(solution)/shard_map/moe/pallas_call | solution.py:397
  76.9 1.6 %copy.10 = bf16[16,4096]{1,0:T(8,128)(2,1)} copy(bf16[16,4096]{1,0:T(8,128)(2,1)} %moe.1) | data formatting | bytes 262144

commit v5 on v4

--- a/solution.py
+++ b/solution.py
@@ -20,7 +20,8 @@
 HALF = 384
 TILE = 256
 GO_WIDTHS = ((512, 1536, 2048), (1024, 1024, 1024, 1024))
-BACK_WIDTHS = ((1024, 3072), (1024, 1024, 1024, 512, 512))
+BACK_WIDTHS = ((1024,3072),(1024,1024,1024,512,256,256))
+STRAIGHT = 2
 MESH = pl.DeviceIdType.MESH
 F32 = jnp.float32
 BF16 = jnp.bfloat16
@@ -110,11 +111,13 @@
         )
         gather[(g, c, q)].start()
 
+    for copy in meta_copies[:NEAR - 1]:
+        copy.start()
     for c in range(len(GO[0])):
         for q in (2, 1, 3):
             ag(0, c, q, tok.at[0], -SOURCES[q])
         if c == 0:
-            for copy in meta_copies:
+            for copy in meta_copies[NEAR - 1:]:
                 copy.start()
 
     def forward(c):
@@ -142,31 +145,37 @@
     spot = jnp.where(slot < 2 * PLANE, spot, -1).astype(F32)[0:1]
     where_to = jnp.where(holder == spot, 1.0, 0.0).astype(BF16)
 
-    for copy in meta_copies:
-        copy.wait_recv()
-    info = meta[...].reshape(NZ * ROWS, 128)
-    named = jnp.zeros((128, 128), F32)
-    weight = jnp.zeros((128, 128), F32)
-    for k in range(8):
-        hit = info[:, k:k + 1] == lane_f
-        named = named + jnp.where(hit, 1.0, 0.0)
-        weight = weight + jnp.where(hit, info[:, 8 + k:9 + k], 0.0)
-    at = dot(named.astype(BF16), where_to)
-    before = jnp.where(((line >> 4) == (lane >> 4)) & (lane < line), 1.0, 0.0).astype(BF16)
-    rank = dot(before, at.astype(BF16))
-    pick = jnp.where(rank == (lane >> 4).astype(F32), at, 0.0)
-    spot_row = lax.broadcasted_iota(jnp.int32, (SOME, 128), 0)
-    spot_slot = lax.broadcasted_iota(jnp.int32, (SOME, 128), 1) >> 4
-    second_rank = spot_row >= NEAR
-
-    def spread(table, g):
-        ours = spot_slot == (spot_row & (NEAR - 1)) + g * NEAR
-        both = jnp.where(second_rank[None], table[PLANE:2 * PLANE][:, None, :], table[0:PLANE][:, None, :])
+    near_rows = NEAR * ROWS
+    spot_row = lax.broadcasted_iota(jnp.int32, (SOME, near_rows), 0)
+    ours = (lax.broadcasted_iota(jnp.int32, (SOME, near_rows), 1) >> 4) == (spot_row & (NEAR - 1))
+    before_line = lax.broadcasted_iota(jnp.int32, (near_rows, near_rows), 0)
+    before_lane = lax.broadcasted_iota(jnp.int32, (near_rows, near_rows), 1)
+    before = jnp.where(
+        ((before_line >> 4) == (before_lane >> 4)) & (before_lane < before_line), 1.0, 0.0
+    ).astype(BF16)
+    rank_lane = (lane[0:near_rows] >> 4).astype(F32)
+
+    def spread(table):
+        turned_table = table.T
+        both = jnp.where(
+            (spot_row >= NEAR)[None], turned_table[PLANE:2 * PLANE][:, None, :], turned_table[0:PLANE][:, None, :]
+        )
         sel[...] = jnp.where(ours[None], both, 0.0)
-        return sel[...].reshape(PLANE * SOME, 128).T[g * 64:(g + 1) * 64]
-
-    picked = pick.T
-    chosen = [spread(picked, g).T.astype(BF16) for g in range(GROUPS)]
+        return sel[...].reshape(PLANE * SOME, near_rows)
+
+    def picks(g):
+        for q in range(max(1, g * NEAR), (g + 1) * NEAR):
+            meta_copies[q - 1].wait_recv()
+        info = meta[g * NEAR:(g + 1) * NEAR].reshape(near_rows, 128)
+        named = jnp.zeros((near_rows, 128), F32)
+        for k in range(8):
+            named = named + jnp.where(info[:, k:k + 1] == lane_f[0:near_rows], 1.0, 0.0)
+        at = dot(named.astype(BF16), where_to)
+        rank = dot(before, at.astype(BF16))
+        return info, jnp.where(rank == rank_lane, at, 0.0)
+
+    tables = [picks(0)]
+    chosen = [spread(tables[0][1]).astype(BF16)]
 
     def go(g, c, p):
         cols = pl.ds(*GO[g][c])
@@ -198,16 +207,21 @@
         for p in range(1, PLANE):
             go(g, c, p).start()
 
-    for c in range(len(GO[0])):
+    dispatch(0, 0)
+    tables.append(picks(1))
+    chosen.append(spread(tables[1][1]).astype(BF16))
+    for c in range(1, len(GO[0])):
         dispatch(0, c)
     dispatch(1, 0)
 
-    high = weight.astype(BF16)
-    low = (weight - high.astype(F32)).astype(BF16)
-    for t, share_of in enumerate((high, low)):
-        table = (dot(share_of, where_to) * pick).T
-        for g in range(GROUPS):
-            comb_t[g, t * 64:(t + 1) * 64] = spread(table, g).astype(BF16)
+    for g, (info, pick) in enumerate(tables):
+        weight = jnp.zeros((near_rows, 128), F32)
+        for k in range(8):
+            weight = weight + jnp.where(info[:, k:k + 1] == lane_f[0:near_rows], info[:, 8 + k:9 + k], 0.0)
+        high = weight.astype(BF16)
+        low = (weight - high.astype(F32)).astype(BF16)
+        for t, share_of in enumerate((high, low)):
+            comb_t[g, t * 64:(t + 1) * 64] = spread(dot(share_of, where_to) * pick).T.astype(BF16)
 
     dispatch(1, 1)
     for load in loads:
@@ -283,11 +297,12 @@
                 finish(g, c - 1)
         finish(g, len(BACK[g]) - 1)
 
-    arrived(0, 0)
-    dispatch(1, 2)
-    arrived(0, 1)
-    arrived(0, 2)
-    dispatch(1, 3)
+    for c in range(len(GO[0])):
+        if c == len(GO[0]) - 1:
+            dispatch(1, 3)
+        arrived(0, c)
+        if c == 0:
+            dispatch(1, 2)
     experts(0)
     for c in range(len(GO[1])):
         arrived(1, c)
@@ -303,6 +318,7 @@
 
     ends = BACK[1]
     last = len(ends) - 1
+    staged = len(ends) - STRAIGHT
     slot_of = {far: q for q, far in enumerate(SOURCES)}
 
     def rs(c, far, dst, by):
@@ -315,12 +331,12 @@
         return rs(c, 1, 0, 1), rs(c, 7, 1, -1)
 
     def rs_far(c):
-        if c == last:
+        if c >= staged:
             return tuple(rs(c, far, dst, far) for far, dst in ((4, 4), (3, 5), (5, 6), (6, 3), (2, 2)))
         return rs(c, 3, 4, 1), rs(c, 5, 5, -1), rs(c, 4, 6, 2)
 
     def rs_second(c):
-        return () if c == last else (rs(c, 2, 2, 2), rs(c, 6, 3, -2))
+        return () if c >= staged else (rs(c, 2, 2, 2), rs(c, 6, 3, -2))
 
     def leave(c, fars):
         start, width = ends[c]
@@ -347,10 +363,10 @@
     def done(c):
         start, width = ends[c]
         cols = slice(start, start + width)
-        for copy in rs_near(c) + (rs_far(c) if c == last else rs_second(c)):
+        for copy in rs_near(c) + (rs_far(c) if c >= staged else rs_second(c)):
             copy.wait_recv()
         total = part[0, :, cols]
-        for i in range(NZ - 1 if c == last else 4):
+        for i in range(NZ - 1 if c >= staged else 4):
             total = total + hop_in[i, :, cols].astype(F32)
         summed[:, cols] = total.astype(BF16)
         written(c).start()
@@ -363,15 +379,22 @@
             copy.start()
     for c in range(last + 1):
         gathered(1, c)
-        leave(c, (4, 3, 5, 6, 2) if c == last else (3, 5, 4))
+        leave(c, (4, 3, 5, 6, 2) if c >= staged else (3, 5, 4))
         for copy in rs_far(c):
             copy.start()
-        if c > 0:
+        if 0 < c < staged - 1:
             middle(c - 1)
-        if c > 1:
-            done(c - 2)
-    done(last - 1)
+        if c > 2 and c - 3 < staged - 2:
+            done(c - 3)
+    middle(staged - 2)
+    for c in range(max(0, last - 2), staged - 2):
+        done(c)
+    middle(staged - 1)
+    for c in range(staged, last):
+        done(c)
+    done(staged - 2)
     done(last)
+    done(staged - 1)
 
     for copy in meta_copies:
         copy.wait_send()
@@ -410,7 +433,7 @@
             pltpu.VMEM((NZ, ROWS, WIDE), BF16),
             pltpu.VMEM((128, 128), F32),
             pltpu.VMEM((NZ, ROWS, 128), F32),
-            pltpu.VMEM((PLANE, SOME, 128), F32),
+            pltpu.VMEM((PLANE, SOME, NEAR * ROWS), F32),
             pltpu.VMEM((GROUPS, 128, lanes), BF16),
             pltpu.VMEM((GROUPS, PLANE, SOME, WIDE), BF16),
             pltpu.VMEM((GROUPS, 2, PLANE, SOME, WIDE), BF16),

time: 79.4 us -> 78.7 us (level)
  Pallas kernels: 76.9 us -> 76.1 us
    pallas_call x1, Pallas kernels: 76.9 us -> 76.1 us  [on_device(): pl.pallas_call(kernel, out_shape=jax.ShapeDtypeStruct(tokens.shape, token...]
where the time goes in v5:
time: 78.7 us; the launch traced here: 77.6 us
  Pallas kernels  76.1 us (97%)
  local copies, waits for them, and re-layouts  1.57 us (2%)
    pallas_call x1, Pallas kernels, on_device(): pl.pallas_call(kernel, out_shape=jax.ShapeDtypeStruct(tokens.shape, token...  76.1 us

profile of v5, /device:TPU:2, one launch (start us, length us, event | category | flops | bytes accessed | tf_op | source)
XLA Modules:
  0.0 77.6 jit_solution(5786397358957588131)
XLA Ops:
  0.0 76.1 %moe.1 = bf16[16,4096]{1,0:T(8,128)(2,1)} custom-call(bf16[16,4096]{1,0:T(8,128)(2,1)} %tokens.1, s32[8,16]{1,0:T(8,128)} %bitcast.4, f32[8,16]{1,0:T(8,128)} %bitcast.5, s32[1,128]{1,0:T(1,128)} %bitcast.6, s32[1,128]{1,0:T(1,128)} %bitcast.7, bf16[1,4096,384]{2,1,0:T(8,128)(2,1)} %w_gate.1, bf16[1,4096,384]{2,1,0:T(8,128)(2,1)} %w_up.1, ...), custom_call_target="tpu_custom_call" | custom-call | tf_op jit(solution)/shard_map/moe/pallas_call | solution.py:420
  76.1 1.6 %copy.10 = bf16[16,4096]{1,0:T(8,128)(2,1)} copy(bf16[16,4096]{1,0:T(8,128)(2,1)} %moe.1) | data formatting | bytes 262144
